TPU v7x, 32 devices: a whole 2x2x4 slice. The times are simulated.
32 devices in a mesh: grp: 2 (over y), freq: 16 (over z, x, core).
Axes of the slice: x: 2, y: 2, z: 4, core: 2. Of those that a mesh axis runs over, the one named last changes fastest.
Arguments:
- source_field: bfloat16 [4, 16, 512, 256], P('grp', 'freq'), parts along dimension 0, may hold values from -6 to 6
- receiver_field: bfloat16 [4, 16, 512, 256], P('grp', 'freq'), parts along dimension 0, may hold values from -6 to 6
- slowness_slabs: bfloat16 [32, 768, 512], P(('grp', 'freq')), parts along dimension 0, may hold values from 0.3984375 to 1.1953125
- slab_map: int32 [4], P('grp'), parts along dimension 0, may hold values from 0 to 15
- reference_gaps: float32 [4, 3], P('grp'), parts along dimension 0, may hold values from 0.1 to 0.3
- reference_index: int32 [4, 512, 256], P('grp'), parts along dimension 0, may hold values from 0 to 1
- frequency_bins: int32 [16], replicated, may hold values from 10 to 120
- shot_corner: int32 [4], P('grp'), parts along dimension 0, may hold values from 0 to 256
Outputs:
- image: float32 [4, 512, 256, 256], P('grp', 'freq'), parts along dimension 0
There are 2 independent parts, one for each index of `grp`. A program takes and returns all parts, laid end to end along the dimension named above; an argument that names none is the same for every part. Nothing has to cross between parts.
All inputs are finite; a program needn't handle non-finite values.
Results may differ from a plain program's by a relative error of at most 0.014.
Values may be sent and summed in bfloat16 or wider, within the bound.
A program may use at most 128 MiB of HBM per device.

v0:
```python
import math

import jax
import jax.numpy as jnp
from jax import lax
from jax.sharding import PartitionSpec as P

LAGS = 256
DEPTHS = 2


cell_width = 0.0125
layer_thick = 0.0125
bin_hertz = 0.5
period_bins = 500
slow_base = 0.3


def spread(block, axis, holder):
    block = jnp.where(lax.axis_index(axis) == holder, block, jnp.zeros_like(block))
    return lax.psum(block, axis)


def transform_table(length, forward):
    grid_steps = jnp.arange(length, dtype=jnp.int32)
    phases = jnp.mod(grid_steps[:, None] * grid_steps[None, :], length).astype(jnp.float32)
    angles = phases * (2.0 * math.pi / length)
    norm_scale = 1.0 / math.sqrt(length)
    cosine = jnp.cos(angles) * norm_scale
    sine_part = jnp.sin(angles) * norm_scale
    if forward:
        cross_term = -sine_part
    else:
        cross_term = sine_part
    return jnp.stack([jnp.stack([cosine, cross_term]), jnp.stack([-cross_term, cosine])]).astype(
        jnp.bfloat16
    )


def wave_numbers(length):
    grid_steps = jnp.arange(length, dtype=jnp.int32)
    folded = jnp.where(grid_steps < length // 2, grid_steps, grid_steps - length).astype(
        jnp.float32
    )
    return folded * (2.0 * math.pi / (length * cell_width))


def lag_table(frequency_bins, lag_count):
    offsets = jnp.arange(lag_count, dtype=jnp.int32) - lag_count // 2
    cycles = jnp.mod(frequency_bins[:, None] * offsets[None, :], period_bins).astype(jnp.float32)
    angles = cycles * (2.0 * math.pi / period_bins)
    return jnp.stack([jnp.cos(angles), -jnp.sin(angles)]).astype(jnp.bfloat16)


def phase_factors(angular, references, squares):
    radicand = (angular * references[:, None, None]) ** 2 - squares[None]
    vertical = jnp.sqrt(jnp.maximum(radicand, 0.0))
    fading = jnp.exp(-jnp.sqrt(jnp.maximum(-radicand, 0.0)) * layer_thick)
    return (fading * jnp.cos(vertical * layer_thick), fading * jnp.sin(vertical * layer_thick))


def rotate(field_pair, turn_angle):
    return jnp.stack(
        [
            jnp.cos(turn_angle) * field_pair[:, 0] - jnp.sin(turn_angle) * field_pair[:, 1],
            jnp.cos(turn_angle) * field_pair[:, 1] + jnp.sin(turn_angle) * field_pair[:, 0],
        ],
        axis=1,
    )


def extrapolate(fields, angular, slowness, references, bracket, direction, tables, squares):
    forward_x, forward_y, inverse_x, inverse_y = tables
    half_done = jnp.einsum(
        "fcxy,cdyk->fdxk", fields, forward_y, preferred_element_type=jnp.float32
    ).astype(jnp.bfloat16)
    spectrum = jnp.einsum(
        "cdxk,fcxy->fdky", forward_x, half_done, preferred_element_type=jnp.float32
    )
    cos_part, sin_part = phase_factors(angular, references, squares)
    turned = direction[:, None, None, None] * sin_part[None]
    real_new = cos_part[None] * spectrum[:, None, 0] - turned * spectrum[:, None, 1]
    imag_new = cos_part[None] * spectrum[:, None, 1] + turned * spectrum[:, None, 0]
    shifted = jnp.stack([real_new, imag_new], axis=2).astype(jnp.bfloat16)
    returned = jnp.einsum(
        "cdxk,fjcxy->fjdky", inverse_x, shifted, preferred_element_type=jnp.float32
    ).astype(jnp.bfloat16)
    refocused = jnp.einsum(
        "fjcxy,cdyk->fjdxk", returned, inverse_y, preferred_element_type=jnp.float32
    )
    lower_pair = bracket == 0
    lower_field = jnp.where(lower_pair, refocused[:, 0], refocused[:, 1])
    upper_field = jnp.where(lower_pair, refocused[:, 1], refocused[:, 2])
    slow_low = jnp.where(lower_pair, references[0], references[1])
    slow_high = jnp.where(lower_pair, references[1], references[2])
    weight = jnp.clip((slowness - slow_low) / (slow_high - slow_low), 0.0, 1.0)
    turn_low = direction[:, None, None] * angular * layer_thick * (slowness - slow_low)[None]
    turn_high = direction[:, None, None] * angular * layer_thick * (slowness - slow_high)[None]
    mixed = (1.0 - weight) * rotate(lower_field, turn_low) + weight * rotate(upper_field, turn_high)
    return mixed.astype(jnp.bfloat16)


def lag_image_depths(cross_spec, lag_weights):
    total_bins = cross_spec.shape[2]
    summed = jnp.einsum(
        "dcwab,cwl->dabl", cross_spec, lag_weights, preferred_element_type=jnp.float32
    )
    return summed * total_bins ** (-0.5)


def cross_product(wave_stack):
    values = wave_stack.astype(jnp.float32)
    real_part = values[0, 0] * values[1, 0] + values[0, 1] * values[1, 1]
    imag_part = values[0, 0] * values[1, 1] - values[0, 1] * values[1, 0]
    return jnp.stack([real_part, imag_part]).astype(jnp.bfloat16)


def shards(
    source_field,
    receiver_field,
    slowness_slabs,
    slab_map,
    reference_gaps,
    reference_index,
    frequency_bins,
    shot_corner,
):
    slots_here = source_field.shape[1]
    rows_x = source_field.shape[2]
    cols_y = source_field.shape[3]
    tables = (
        transform_table(rows_x, True),
        transform_table(cols_y, True),
        transform_table(rows_x, False),
        transform_table(cols_y, False),
    )
    wave_x = wave_numbers(rows_x)
    wave_y = wave_numbers(cols_y)
    squares = wave_x[:, None] ** 2 + wave_y[None, :] ** 2
    freq_rank = lax.axis_index("freq")
    my_bins = lax.dynamic_slice_in_dim(frequency_bins, freq_rank * slots_here, slots_here)
    omegas = my_bins.astype(jnp.float32) * (2.0 * math.pi * bin_hertz)
    lag_weights = lag_table(frequency_bins, LAGS)
    direction = jnp.array([1.0, -1.0], jnp.float32)
    wave_stack = jnp.stack([source_field, receiver_field])
    slab_count = slowness_slabs.shape[0]
    corner_x = shot_corner[0]
    corner_y = shot_corner[1]
    crosses = []
    for depth_step in range(DEPTHS):
        global_slab = slab_map[depth_step]
        owner_rank = global_slab // slab_count
        local_pick = global_slab % slab_count
        own_window = lax.dynamic_slice(
            slowness_slabs, (local_pick, corner_x, corner_y), (1, rows_x, cols_y)
        )[0]
        window = spread(own_window, "freq", owner_rank)
        slowness = window.astype(jnp.float32)
        references = slow_base + jnp.cumsum(reference_gaps[depth_step])
        bracket = reference_index[depth_step]
        stepped = [
            extrapolate(
                wave_stack[:, :, 0],
                omegas[0],
                slowness,
                references,
                bracket,
                direction,
                tables,
                squares,
            )
        ]
        wave_stack = jnp.stack(stepped, axis=2)
        crosses.append(cross_product(wave_stack))
    all_crosses = jnp.stack(crosses)
    return lag_image_depths(
        lax.all_to_all(all_crosses, "freq", split_axis=3, concat_axis=2, tiled=True), lag_weights
    )


def solution(mesh):
    placed = (
        P("grp", "freq", None, None),
        P("grp", "freq", None, None),
        P(("grp", "freq"), None, None),
        P("grp"),
        P("grp", None),
        P("grp", None, None),
        P(),
        P("grp"),
    )
    return jax.shard_map(
        shards, mesh=mesh, in_specs=placed, out_specs=P("grp", "freq", None, None), check_vma=False
    )
```

profile of v0, /device:TPU:9, one launch (start us, length us, event | category | flops | bytes accessed | tf_op | source)
XLA Modules:
  0.0 221.5 jit_solution(4472801695292932038)
XLA Ops:
  6.5 1.3 fusion.162
  14.3 2.0 select_bitcast_fusion
  16.3 4.4 %negate_convert_fusion = (bf16[1,512,512]{2,1,0:T(8,128)(2,1)S(1)}, bf16[1,512,512]{2,1,0:T(8,128)(2,1)S(1)}) fusion(), kind=kLoop, calls=%fused_computation.150 | loop fusion | flops 4980736 | bytes 1048576 | tf_op jit(solution)/shard_map/convert.25
  20.7 4.0 %fusion.115 = bf16[1,512,512]{2,1,0:T(8,128)(2,1)S(1)} fusion(), kind=kLoop, calls=%fused_computation.157 | loop fusion | flops 4194304 | bytes 524288 | tf_op jit(solution)/shard_map/convert.21
  28.5 1.8 fusion.89
  31.3 3.7 %convolution_bitcast_fusion.1 = f32[2,2,512,256]{2,3,1,0:T(8,128)S(1)} fusion(bf16[1,2,512,512]{3,2,0,1:T(8,128)(2,1)S(1)} %get-tuple-element.38, bf16[1,2,512,512]{3,2,0,1:T(8,128)(2,1)} %get-tuple-element.49, bf16[1,2,1,512,256]{4,3,1,0,2:T(8,128)(2,1)} %bitcast.250, bf16[1,2,1,512,256]{4,3,1,0,2:T(8,128)(2,1)} %bitcast.251, ...), kind=kOutput, calls=%fused_computation.63 | convolution fusion | flops 1618477056 | bytes 5767168 | tf_op jit(solution)/shard_map/cdxk,fcxy->fdky/dot_general | solution.py:77
  35.9 14.4 %fusion.59 = (f32[3,512,256]{1,2,0:T(8,128)}, f32[3,512,256]{1,2,0:T(8,128)}, f32[3,512,256]{1,2,0:T(8,128)S(1)}, f32[3,512,256]{1,2,0:T(8,128)S(1)}) fusion(f32[3]{0:T(128)S(1)} %get-tuple-element.73, f32[512,256]{0,1:T(8,128)S(1)} %broadcast_add_fusion, f32[3]{0:T(128)S(1)} %get-tuple-element.85), kind=kLoop, calls=%fused_computation.81 | loop fusion | flops 7077888 | bytes 6815768 | tf_op jit(solution)/shard_map/mul | solution.py:59
  51.5 9.4 %fusion.27 = f32[2,3,2,512,256]{3,4,1,0,2:T(8,128)} fusion(bf16[2,3,1,512,256]{3,4,2,1,0:T(8,128)(2,1)S(1)} %get-tuple-element.18, bf16[2,3,1,512,256]{3,4,2,1,0:T(8,128)(2,1)S(1)} %get-tuple-element.17, bf16[1,2,512,512]{3,2,1,0:T(8,128)(2,1)} %get-tuple-element.50, bf16[1,2,512,512]{3,2,1,0:T(8,128)(2,1)} %get-tuple-element.37, ...), kind=kOutput, calls=%fused_computation.31 | convolution fusion | flops 4844158976 | bytes 12058624 | tf_op jit(solution)/shard_map/fjcxy,cdyk->fjdxk/dot_general | solution.py:88
  61.5 46.2 %all-reduce.3.cloned.1.call-done = (bf16[512,256]{1,0:T(8,128)(2,1)}, bf16[512,256]{1,0:T(8,128)(2,1)}) async-done(((bf16[512,256]{1,0:T(8,128)(2,1)}, bf16[512,256]{1,0:T(8,128)(2,1)}), (bf16[512,256]{1,0:T(8,128)(2,1)}, bf16[512,256]{1,0:T(8,128)(2,1)})) %all-reduce.3.cloned.1.call-update) | async-done | bytes 524304 | tf_op jit(solution)/shard_map/psum | solution.py:21
  107.8 6.4 %broadcast_subtract_fusion = (f32[512,256]{1,0:T(8,128)}, pred[512,256]{1,0:T(8,128)(4,1)S(1)}, f32[512,256]{1,0:T(8,128)S(1)}, pred[512,256]{1,0:T(8,128)(4,1)S(1)}) fusion(f32[]{:T(128)} %bitcast.64, f32[]{:T(128)} %bitcast.63, f32[]{:T(128)} %bitcast.62, bf16[512,256]{1,0:T(8,128)(2,1)} %get-tuple-element.6, s32[2,512,256]{2,1,0:T(8,128)} %param.14, ...), kind=kLoop, calls=%fused_computation.202 | loop fusion | flops 2359296 | bytes 2883608 | tf_op jit(solution)/shard_map/sub | solution.py:99
  114.4 2.2 select_subtract_fusion.5
  116.8 3.1 %fusion.121 = (f32[512,256]{1,0:T(8,128)}, f32[512,256]{1,0:T(8,128)}, f32[512,256]{1,0:T(8,128)}) fusion(pred[512,256]{1,0:T(8,128)(4,1)S(1)} %get-tuple-element.8, f32[]{:T(128)} %bitcast.64, f32[]{:T(128)} %bitcast.63, f32[]{:T(128)} %bitcast.62, bf16[512,256]{1,0:T(8,128)(2,1)S(1)} %copy-done.9), kind=kLoop, calls=%fused_computation.167 | loop fusion | flops 1048576 | bytes 1966092 | tf_op jit(solution)/shard_map/jit(clip)/min | solution.py:96
  124.0 3.7 %fusion.35 = (f32[2,2,512,256]{2,3,0,1:T(8,128)S(1)}, f32[2,2,512,256]{2,3,0,1:T(8,128)S(1)}) fusion(f32[2,3,2,512,256]{3,4,1,0,2:T(8,128)} %fusion.27, pred[512,256]{0,1:T(8,128)(4,1)S(1)} %copy.57), kind=kLoop, calls=%fused_computation.45 | loop fusion | flops 1048576 | bytes 10616832 | tf_op jit(solution)/shard_map/jit(_where)/select_n | solution.py:92
  127.8 9.0 %fusion.100 = (f32[2,1,512,256]{2,3,0,1:T(8,128)S(1)}, f32[2,1,512,256]{2,3,0,1:T(8,128)S(1)}, f32[2,1,512,256]{2,3,0,1:T(8,128)S(1)}, f32[2,1,512,256]{2,3,0,1:T(8,128)}) fusion(f32[2,2,512,256]{2,3,0,1:T(8,128)S(1)} %get-tuple-element.13, f32[512,256]{0,1:T(8,128)S(1)} %copy-done, f32[2]{0:T(128)S(1)} %multiply_multiply_fusion.4, ...), kind=kLoop, calls=%fused_computation.133 | loop fusion | flops 3670016 | bytes 9437192 | tf_op jit(solution)/shard_map/sub | solution.py:65
  136.8 5.6 %convolution_bitcast_fusion = f32[2,2,512,256]{2,3,1,0:T(8,128)} fusion(bf16[1,2,512,512]{3,2,0,1:T(8,128)(2,1)} %copy-done.14, bf16[1,2,512,512]{3,2,0,1:T(8,128)(2,1)} %get-tuple-element.49, bf16[1,2,256,256]{2,3,0,1:T(8,128)(2,1)} %get-tuple-element.58, bf16[1,2,256,256]{2,3,0,1:T(8,128)(2,1)} %get-tuple-element.61, ...), kind=kOutput, calls=%fused_computation.62 | convolution fusion | flops 1619525632 | bytes 9961472 | tf_op jit(solution)/shard_map/cdxk,fcxy->fdky/dot_general | solution.py:77
  142.4 2.1 fusion.106
  149.6 3.6 %fusion.11 = bf16[2,3,2,512,256,1]{3,4,2,1,0,5:T(8,128)(2,1)S(1)} fusion(bf16[2,3,1,512,256]{3,4,2,1,0:T(8,128)(2,1)S(1)} %get-tuple-element.16, bf16[2,3,1,512,256]{3,4,2,1,0:T(8,128)(2,1)S(1)} %get-tuple-element.15, bf16[1,2,512,512]{3,2,1,0:T(8,128)(2,1)S(1)} %copy-done.13, bf16[1,2,512,512]{3,2,1,0:T(8,128)(2,1)S(1)} %copy-done.12), kind=kOutput, calls=%fused_computation.17 | convolution fusion | flops 3233284096 | bytes 8388608 | tf_op jit(solution)/shard_map/cdxk,fjcxy->fjdky/dot_general | solution.py:85
  153.2 4.5 %fusion.24 = f32[2,3,2,512,256]{3,4,0,2,1:T(8,128)} fusion(bf16[2,3,2,512,256,1]{3,4,2,1,0,5:T(8,128)(2,1)S(1)} %fusion.11, bf16[1,2,256,256]{2,3,1,0:T(8,128)(2,1)S(1)} %copy-done.11, bf16[1,2,256,256]{2,3,1,0:T(8,128)(2,1)S(1)} %get-tuple-element.57), kind=kOutput, calls=%fused_computation.30 | convolution fusion | flops 1610874880 | bytes 9961472 | tf_op jit(solution)/shard_map/fjcxy,cdyk->fjdxk/dot_general | solution.py:88
  159.2 3.7 %fusion.33 = (f32[2,2,512,256]{2,3,0,1:T(8,128)S(1)}, f32[2,2,512,256]{2,3,0,1:T(8,128)S(1)}) fusion(f32[2,3,2,512,256]{3,4,0,2,1:T(8,128)} %fusion.24, pred[512,256]{0,1:T(8,128)(4,1)S(1)} %copy.69), kind=kLoop, calls=%fused_computation.40 | loop fusion | flops 1048576 | bytes 10616832 | tf_op jit(solution)/shard_map/jit(_where)/select_n | solution.py:92
  162.9 8.0 %fusion.95 = (f32[2,1,1,512,256]{3,4,0,2,1:T(8,128)S(1)}, f32[2,1,1,512,256]{3,4,0,2,1:T(8,128)S(1)}, f32[2,1,1,512,256]{3,4,0,2,1:T(8,128)S(1)}, f32[2,1,1,512,256]{3,4,0,2,1:T(8,128)S(1)}) fusion(f32[2,2,512,256]{2,3,0,1:T(8,128)S(1)} %get-tuple-element.11, f32[512,256]{0,1:T(8,128)S(1)} %copy.68, f32[2]{0:T(128)S(1)} %multiply_multiply_fusion.4, ...), kind=kLoop, calls=%fused_computation.128 | loop fusion | flops 3670016 | bytes 9437192 | tf_op jit(solution)/shard_map/stack | solution.py:63
  172.6 2.1 copy.79
  174.7 6.5 %all-to-all-start = ((bf16[2,2,1,512,256]{4,0,2,1,3:T(2,128)(2,1)}), bf16[2,2,1,512,256]{4,0,2,1,3:T(2,128)(2,1)S(1)}, u32[]{:S(2)}, u32[]{:S(2)}) async-start(bf16[2,2,1,512,256]{4,0,2,1,3:T(2,128)(2,1)} %copy.79), calls=%async_computation | async-start | bytes 2097152 | tf_op jit(solution)/shard_map/all_to_all | solution.py:177
  181.3 24.8 %all-to-all-done = bf16[2,2,1,512,256]{4,0,2,1,3:T(2,128)(2,1)S(1)} async-done(((bf16[2,2,1,512,256]{4,0,2,1,3:T(2,128)(2,1)}), bf16[2,2,1,512,256]{4,0,2,1,3:T(2,128)(2,1)S(1)}, u32[]{:S(2)}, u32[]{:S(2)}) %all-to-all-start) | async-done | bytes 1048608 | tf_op jit(solution)/shard_map/all_to_all | solution.py:177
  206.1 8.6 %bitcast_multiply_fusion = f32[2,32,256,256]{3,2,1,0:T(8,128)} fusion(bf16[2,2,16,32,256]{4,0,1,3,2:T(2,128)(2,1)S(1)} %bitcast.249, bf16[1,16,256]{2,1,0:T(8,128)(2,1)S(1)} %get-tuple-element.64, bf16[1,16,256]{2,1,0:T(8,128)(2,1)S(1)} %get-tuple-element.63), kind=kOutput, calls=%fused_computation | convolution fusion | flops 272637952 | bytes 17842176 | tf_op jit(solution)/shard_map/dcwab,cwl->dabl/dot_general | solution.py:105
  (75 shorter events, 21.0 us)
Async XLA Ops:
  6.5 20.3 %copy-start.18 = (s32[16]{0:T(128)S(1)}, s32[16]{0:T(128)}, u32[]{:S(2)}) copy-start(s32[16]{0:T(128)} %param.15) | copy-start | bytes 196
  6.5 21.6 %copy-start.17 = (f32[2,3]{1,0:T(2,128)S(1)}, f32[2,3]{1,0:T(2,128)}, u32[]{:S(2)}) copy-start(f32[2,3]{1,0:T(2,128)} %param.13) | copy-start | bytes 76
  6.5 101.2 %all-reduce.3.cloned.1.call-start = ((), (), s32[]{:S(2)}) async-start(), calls=%async_computation.1 | async-start | bytes 1048576 | tf_op jit(solution)/shard_map/psum | solution.py:21
  30.3 4.7 %copy-start.14 = (bf16[1,2,512,512]{3,2,0,1:T(8,128)(2,1)}, bf16[1,2,512,512]{3,2,0,1:T(8,128)(2,1)S(1)}, u32[]{:S(2)}) copy-start(bf16[1,2,512,512]{3,2,0,1:T(8,128)(2,1)S(1)} %get-tuple-element.38) | copy-start | bytes 3145732
  35.9 14.4 %copy-start.16 = (f32[2]{0:T(128)S(1)}, f32[2]{0:T(128)}, u32[]{:S(2)}) copy-start(f32[2]{0:T(128)} %constant.135.clone) | copy-start | bytes 28
  107.8 6.7 %copy-start.10 = (bf16[512,256]{1,0:T(8,128)(2,1)S(1)}, bf16[512,256]{1,0:T(8,128)(2,1)}, u32[]{:S(2)}) copy-start(bf16[512,256]{1,0:T(8,128)(2,1)} %get-tuple-element.5) | copy-start | bytes 786436
  107.8 9.1 %copy-start.9 = (bf16[512,256]{1,0:T(8,128)(2,1)S(1)}, bf16[512,256]{1,0:T(8,128)(2,1)}, u32[]{:S(2)}) copy-start(bf16[512,256]{1,0:T(8,128)(2,1)} %get-tuple-element.6) | copy-start | bytes 786436
  124.0 3.7 %copy-start = (f32[512,256]{0,1:T(8,128)S(1)}, f32[512,256]{0,1:T(8,128)}, u32[]{:S(2)}) copy-start(f32[512,256]{0,1:T(8,128)} %copy.56) | copy-start | bytes 1572868
  124.0 3.8 %copy-start.1 = (f32[512,256]{0,1:T(8,128)S(1)}, f32[512,256]{0,1:T(8,128)}, u32[]{:S(2)}) copy-start(f32[512,256]{0,1:T(8,128)} %copy.66) | copy-start | bytes 1572868
  144.5 1.7 copy-start.2
  146.2 1.4 copy-start.7
  146.2 1.9 copy-start.8
  148.1 1.2 copy-start.12
  148.1 1.5 copy-start.13
  149.6 3.6 %copy-start.11 = (bf16[1,2,256,256]{2,3,1,0:T(8,128)(2,1)S(1)}, bf16[1,2,256,256]{2,3,1,0:T(8,128)(2,1)}, u32[]{:S(2)}) copy-start(bf16[1,2,256,256]{2,3,1,0:T(8,128)(2,1)} %get-tuple-element.62) | copy-start | bytes 786436
  153.2 4.5 %copy-start.6 = (f32[512,256]{1,0:T(8,128)S(1)}, f32[512,256]{1,0:T(8,128)}, u32[]{:S(2)}) copy-start(f32[512,256]{1,0:T(8,128)} %get-tuple-element.53) | copy-start | bytes 1572868
  153.2 4.7 %copy-start.5 = (f32[512,256]{1,0:T(8,128)S(1)}, f32[512,256]{1,0:T(8,128)}, u32[]{:S(2)}) copy-start(f32[512,256]{1,0:T(8,128)} %get-tuple-element.52) | copy-start | bytes 1572868
  157.8 1.0 copy-start.4
  157.8 1.2 copy-start.3
  171.5 1.0 copy-start.15
  174.7 31.4 %all-to-all-start = ((bf16[2,2,1,512,256]{4,0,2,1,3:T(2,128)(2,1)}), bf16[2,2,1,512,256]{4,0,2,1,3:T(2,128)(2,1)S(1)}, u32[]{:S(2)}, u32[]{:S(2)}) async-start(bf16[2,2,1,512,256]{4,0,2,1,3:T(2,128)(2,1)} %copy.79), calls=%async_computation | async-start | bytes 2097152 | tf_op jit(solution)/shard_map/all_to_all | solution.py:177
Sparse Core Ops, SparseCore 0:
  16.4 91.2 all-reduce.2
where the time goes:
time: 222 us; the launch traced here: 221 us
  other arithmetic  72.8 us (33%)
  waiting for transfers between devices  71 us (32%)
  matrix products  35.3 us (16%)
  between operations  19.5 us (9%)
  local copies, waits for them, and re-layouts  16.4 us (7%)
  starting transfers between devices  6.48 us (3%)
    psum x1, waiting for transfers between devices, spread(): return lax.psum(block, axis)  46.2 us
    all_to_all x1, waiting for transfers between devices, shards(): lax.all_to_all(all_crosses, 'freq', split_axis=3, concat_axis=2, tiled=True)  24.8 us
    another operation x11, other arithmetic  14.5 us
    mul x1, other arithmetic, phase_factors(): fading * jnp.cos(vertical * layer_thick)  14.4 us
    dot_general x2, matrix products, extrapolate(): jnp.einsum('fjcxy,cdyk->fjdxk', returned, inverse_y, preferred_element_ty...  13.9 us
    dot_general x2, matrix products, extrapolate(): jnp.einsum('cdxk,fcxy->fdky', forward_x, half_done, preferred_element_typ...  9.22 us
    sub x1, other arithmetic, rotate(): jnp.cos(turn_angle) * field_pair[:, 0]  9.01 us
    dot_general x1, matrix products, lag_image_depths(): jnp.einsum('dcwab,cwl->dabl', cross_spec, lag_weights, preferred_element_...  8.56 us
  transfers between devices with their start and end apart: 2, of which 2 were waited for; matrix products, arithmetic and copies ran while one was open for 20% of the time, Pallas kernels for 0%

commit v1 on v0

v1 whole, which is shorter than its diff:
```python
import functools
import math

import jax
import jax.numpy as jnp
import numpy as np
from jax import lax
from jax.experimental import pallas as pl
from jax.experimental.pallas import tpu as pltpu
from jax.sharding import PartitionSpec as P

LAGS = 256

cell_width = 0.0125
layer_thick = 0.0125
bin_hertz = 0.5
period_bins = 500
slow_base = 0.3
chunk = 16
tile = 256


def transform_block(length):
    steps = np.arange(length, dtype=np.int64)
    phases = np.mod(steps[:, None] * steps[None, :], length).astype(np.float32)
    angles = phases * np.float32(2.0 * math.pi / length)
    scale = np.float32(1.0 / math.sqrt(length))
    cosine = np.cos(angles) * scale
    sine = np.sin(angles) * scale
    return np.block([[cosine, -sine], [sine, cosine]]).astype(jnp.bfloat16)


def lag_table(frequency_bins, lag_count):
    offsets = jnp.arange(lag_count, dtype=jnp.int32) - lag_count // 2
    cycles = jnp.mod(frequency_bins[:, None] * offsets[None, :], period_bins).astype(jnp.float32)
    angles = cycles * (2.0 * math.pi / period_bins)
    return jnp.stack([jnp.cos(angles), -jnp.sin(angles)]).astype(jnp.bfloat16)


def sin_cos(angle):
    turns = jnp.floor(angle * (2.0 / math.pi) + 0.5)
    rest = angle - turns * 1.5707855224609375
    rest = rest - turns * 1.0804334124e-05
    quarter = turns.astype(jnp.int32)
    square = rest * rest
    sine = rest + rest * square * (
        -1.6666654611e-1 + square * (8.3321608736e-3 + square * -1.9515295891e-4)
    )
    cosine = (
        1.0
        - 0.5 * square
        + square * square
        * (4.166664568298827e-2 + square * (-1.388731625493765e-3 + square * 2.443315711809948e-5))
    )
    odd = (quarter & 1) == 1
    sine_out = jnp.where(odd, cosine, sine)
    cosine_out = jnp.where(odd, sine, cosine)
    sine_out = jnp.where((quarter & 2) == 2, -sine_out, sine_out)
    cosine_out = jnp.where(((quarter + 1) & 2) == 2, -cosine_out, cosine_out)
    return sine_out, cosine_out


def folded_square(index, length):
    folded = jnp.where(index < length // 2, index, index - length).astype(jnp.float32)
    wave = folded * (2.0 * math.pi / (length * cell_width))
    return wave * wave


def step_kernel(
    scalars, source, receiver, table_x, table_y, slow, bracket,
    out_source, out_receiver, cross,
    half, spectrum, shifted, returned, refocused,
):
    rows_x, cols_y = slow.shape
    angular = scalars[0]
    fields = (source, receiver)
    signs = (1.0, -1.0)

    def lanes(which):
        return pl.ds(which * cols_y, cols_y)

    for which, field in enumerate(fields):
        for start in range(0, rows_x, tile):
            rows = pl.ds(start, tile)
            both = jnp.concatenate([field[0, rows, :], field[1, rows, :]], axis=1)
            out = jnp.dot(both, table_y[...], preferred_element_type=jnp.float32)
            out = out.astype(jnp.bfloat16)
            half[rows, lanes(which)] = out[:, :cols_y]
            half[pl.ds(rows_x + start, tile), lanes(which)] = out[:, cols_y:]

    @pl.loop(0, 2 * rows_x // tile)
    def _(number):
        rows = pl.ds(pl.multiple_of(number * tile, tile), tile)
        spectrum[rows, :] = jnp.dot(
            table_x[rows, :], half[...], preferred_element_type=jnp.float32
        )

    for ref in range(3):
        @pl.loop(0, rows_x // chunk)
        def _(number):
            start = pl.multiple_of(number * chunk, chunk)
            rows = pl.ds(start, chunk)
            low_rows = pl.ds(rows_x + start, chunk)
            row_index = lax.broadcasted_iota(jnp.int32, (chunk, cols_y), 0) + start
            col_index = lax.broadcasted_iota(jnp.int32, (chunk, cols_y), 1)
            squares = folded_square(row_index, rows_x) + folded_square(col_index, cols_y)
            reach = angular * scalars[1 + ref]
            radicand = reach * reach - squares
            depth = jnp.sqrt(jnp.abs(radicand)) * layer_thick
            moving = radicand > 0.0
            fading = jnp.exp(jnp.where(moving, 0.0, -depth))
            sine, cosine = sin_cos(jnp.where(moving, depth, 0.0) - reach * layer_thick)
            cosine = fading * cosine
            sine = fading * sine
            for which in range(2):
                turned = signs[which] * sine
                real = spectrum[rows, lanes(which)]
                imag = spectrum[low_rows, lanes(which)]
                shifted[rows, lanes(which)] = (cosine * real - turned * imag).astype(jnp.bfloat16)
                shifted[low_rows, lanes(which)] = (-(cosine * imag + turned * real)).astype(
                    jnp.bfloat16
                )

        @pl.loop(0, 2 * rows_x // tile)
        def _(number):
            rows = pl.ds(pl.multiple_of(number * tile, tile), tile)
            returned[rows, :] = jnp.dot(
                table_x[rows, :], shifted[...], preferred_element_type=jnp.float32
            ).astype(jnp.bfloat16)

        for which in range(2):
            for start in range(0, rows_x, tile):
                rows = pl.ds(start, tile)
                both = jnp.concatenate(
                    [
                        returned[rows, lanes(which)],
                        returned[pl.ds(rows_x + start, tile), lanes(which)],
                    ],
                    axis=1,
                )
                refocused[ref, which, rows, :] = jnp.dot(
                    both, table_y[...], preferred_element_type=jnp.float32
                )

    @pl.loop(0, rows_x // chunk)
    def _(number):
        rows = pl.ds(pl.multiple_of(number * chunk, chunk), chunk)
        slowness = slow[rows, :].astype(jnp.float32)
        lower = bracket[rows, :] == 0
        slow_low = jnp.where(lower, scalars[1], scalars[2])
        slow_gap = jnp.where(lower, scalars[4], scalars[5])
        weight = jnp.clip((slowness - slow_low) / slow_gap, 0.0, 1.0)
        sine, cosine = sin_cos((angular * layer_thick) * slowness)
        rounded = []
        for which, out in enumerate((out_source, out_receiver)):
            mixed = []
            for part in range(2):
                first = refocused[0, which, rows, lanes(part)]
                second = refocused[1, which, rows, lanes(part)]
                third = refocused[2, which, rows, lanes(part)]
                low = jnp.where(lower, first, second)
                high = jnp.where(lower, second, third)
                mixed.append((1.0 - weight) * low + weight * high)
            turned = signs[which] * sine
            real = (cosine * mixed[0] + turned * mixed[1]).astype(jnp.bfloat16)
            imag = (turned * mixed[0] - cosine * mixed[1]).astype(jnp.bfloat16)
            out[0, rows, :] = real
            out[1, rows, :] = imag
            rounded.append((real.astype(jnp.float32), imag.astype(jnp.float32)))
        (sr, si), (rr, ri) = rounded
        cross[0, rows, :] = (sr * rr + si * ri).astype(jnp.bfloat16)
        cross[1, rows, :] = (sr * ri - si * rr).astype(jnp.bfloat16)


def depth_step(scalars, source, receiver, table_x, table_y, slow, bracket):
    rows_x, cols_y = slow.shape
    field = jax.ShapeDtypeStruct((2, rows_x, cols_y), jnp.bfloat16)
    vmem = pl.BlockSpec(memory_space=pltpu.VMEM)
    flops = 2 * 4 * (2 * rows_x) * (2 * rows_x + 2 * cols_y) * 2 * cols_y
    return pl.pallas_call(
        step_kernel,
        out_shape=(field, field, field),
        in_specs=[pl.BlockSpec(memory_space=pltpu.SMEM)] + [vmem] * 6,
        out_specs=(vmem,) * 3,
        scratch_shapes=[
            pltpu.VMEM((2 * rows_x, 2 * cols_y), jnp.bfloat16),
            pltpu.VMEM((2 * rows_x, 2 * cols_y), jnp.float32),
            pltpu.VMEM((2 * rows_x, 2 * cols_y), jnp.bfloat16),
            pltpu.VMEM((2 * rows_x, 2 * cols_y), jnp.bfloat16),
            pltpu.VMEM((3, 2, rows_x, 2 * cols_y), jnp.float32),
        ],
        cost_estimate=pl.CostEstimate(
            flops=3 * flops, bytes_accessed=8 * 1024 * 1024, transcendentals=0
        ),
        compiler_params=pltpu.CompilerParams(vmem_limit_bytes=40 * 1024 * 1024),
    )(scalars, source, receiver, table_x, table_y, slow, bracket)


def share_kernel(devices, mine, out, pair, part, parts, total, pair_sems, send_sems, recv_sems):
    chips = devices // 2
    me = lax.axis_index("freq")
    grp = lax.axis_index("grp")
    core = lax.rem(me, 2)
    chip = me // 2
    other = 1 - core

    def device(where, side):
        return (grp, where * 2 + side)

    barrier = pltpu.get_barrier_semaphore()
    pl.semaphore_signal(
        barrier, inc=1, device_id=device(chip, other), device_id_type=pl.DeviceIdType.MESH
    )
    for hop in range(1, chips):
        pl.semaphore_signal(
            barrier, inc=1, device_id=device(lax.rem(chip + hop, chips), core),
            device_id_type=pl.DeviceIdType.MESH,
        )
    pl.semaphore_wait(barrier, chips)

    def copy(source, target, send, recv, where, side):
        return pltpu.make_async_remote_copy(
            src_ref=source, dst_ref=target, send_sem=send, recv_sem=recv,
            device_id=device(where, side), device_id_type=pl.DeviceIdType.MESH,
        )

    first = copy(mine.at[other], pair, pair_sems.at[0], pair_sems.at[1], chip, other)
    first.start()
    first.wait()
    part[...] = mine[core] + pair[...]
    sends = []
    for hop in range(1, chips):
        to = lax.rem(chip + hop, chips)
        sends.append(
            copy(part.at[to], parts.at[hop], send_sems.at[0, hop], recv_sems.at[0, hop], to, core)
        )
        sends[-1].start()
    summed = part[chip]
    for hop in range(1, chips):
        sends[hop - 1].wait()
        summed = summed + parts[hop]
    total[...] = summed
    out[core, chip] = summed
    sends = []
    for hop in range(1, chips):
        to = lax.rem(chip + hop, chips)
        sends.append(
            copy(
                total, out.at[core, chip], send_sems.at[1, hop], recv_sems.at[1, hop], to, core
            )
        )
        sends[-1].start()
    for each in sends:
        each.wait()
    last = copy(out.at[core], out.at[core], pair_sems.at[2], pair_sems.at[3], chip, other)
    last.start()
    last.wait()


def share(blocks, devices):
    chips = devices // 2
    whole = blocks.shape
    rows = math.prod(whole[:-1]) // devices
    held = (2, chips, rows, whole[-1])
    vmem = pl.BlockSpec(memory_space=pltpu.VMEM)
    shared = pl.pallas_call(
        functools.partial(share_kernel, devices),
        out_shape=jax.ShapeDtypeStruct(held, blocks.dtype),
        in_specs=[vmem],
        out_specs=vmem,
        scratch_shapes=[
            pltpu.VMEM(held[1:], blocks.dtype),
            pltpu.VMEM(held[1:], blocks.dtype),
            pltpu.VMEM(held[1:], blocks.dtype),
            pltpu.VMEM(held[2:], blocks.dtype),
            pltpu.SemaphoreType.DMA((4,)),
            pltpu.SemaphoreType.DMA((2, chips)),
            pltpu.SemaphoreType.DMA((2, chips)),
        ],
        compiler_params=pltpu.CompilerParams(collective_id=0, has_side_effects=True),
    )(blocks.reshape(held))
    return shared.reshape(whole)


def shards(
    devices,
    source_field,
    receiver_field,
    slowness_slabs,
    slab_map,
    reference_gaps,
    reference_index,
    frequency_bins,
    shot_corner,
):
    rows_x = source_field.shape[2]
    cols_y = source_field.shape[3]
    depths = slab_map.shape[0]
    table_x = jnp.asarray(transform_block(rows_x).T)
    table_y = jnp.asarray(transform_block(cols_y))
    freq_rank = lax.axis_index("freq")
    slab_count = slowness_slabs.shape[0]
    angular = lax.dynamic_index_in_dim(frequency_bins, freq_rank, 0, False).astype(
        jnp.float32
    ) * (2.0 * math.pi * bin_hertz)
    lag_weights = lag_table(frequency_bins, LAGS)
    windows = []
    for depth in range(depths):
        slab = slab_map[depth]
        window = lax.dynamic_slice(
            slowness_slabs,
            (slab % slab_count, shot_corner[0], shot_corner[1]),
            (1, rows_x, cols_y),
        )[0]
        windows.append(jnp.where(slab // slab_count == freq_rank, window, 0))
    slow = share(jnp.stack(windows), devices)
    source = source_field[:, 0]
    receiver = receiver_field[:, 0]
    images = []
    scale = frequency_bins.shape[0] ** (-0.5)
    crosses = []
    for depth in range(depths):
        references = slow_base + jnp.cumsum(reference_gaps[depth])
        scalars = jnp.concatenate([angular[None], references, references[1:] - references[:-1]])
        source, receiver, cross = depth_step(
            scalars, source, receiver, table_x, table_y, slow[depth], reference_index[depth]
        )
        crosses.append(
            lax.all_to_all(cross[:, None], "freq", split_axis=2, concat_axis=1, tiled=True)
        )
    return (
        jnp.einsum(
            "dcwab,cwl->dabl", jnp.stack(crosses), lag_weights, preferred_element_type=jnp.float32
        )
        * scale
    )


def solution(mesh):
    placed = (
        P("grp", "freq", None, None),
        P("grp", "freq", None, None),
        P(("grp", "freq"), None, None),
        P("grp"),
        P("grp", None),
        P("grp", None, None),
        P(),
        P("grp"),
    )
    return jax.shard_map(
        functools.partial(shards, mesh.shape["freq"]),
        mesh=mesh,
        in_specs=placed,
        out_specs=P("grp", "freq", None, None),
        check_vma=False,
    )
```

time: 222 us -> 123 us (0.55)
  other arithmetic: 72.8 us -> 2.78 us
  Pallas kernels: 0 us -> 59.2 us
  waiting for transfers between devices: 71 us -> 12.5 us
  matrix products: 35.3 us -> 8.55 us
  between operations: 19.5 us -> 5.85 us
  starting transfers between devices: 6.48 us -> 11.9 us
  local copies, waits for them, and re-layouts: 16.4 us -> 19.9 us
    pallas_call x0 -> x3, Pallas kernels: none -> 59.2 us  [the longest x2 36.3 us: depth_step(): pl.pallas_call(step_kernel, out_shape=(field, field, field), in_specs=[pl...]
    psum x1 -> x0, waiting for transfers between devices: 46.2 us -> none  [spread(): return lax.psum(block, axis)]
    dot_general x6 -> x1, matrix products: 35.3 us -> 8.55 us  [shards(): jnp.einsum('dcwab,cwl->dabl', jnp.stack(crosses), lag_weights, preferred_...]
    another operation x15 -> x4, other arithmetic: 25.4 us -> 1.35 us  [the longest x1 0.84 us: shards(): slow = share(jnp.stack(windows), devices)]
    sub x3 -> x2, other arithmetic: 17.6 us -> 0.15 us  [shards(): references[1:] - references[:-1]]
    mul x2 -> x0, other arithmetic: 14.4 us -> none  [the longest x1 14.4 us: phase_factors(): fading * jnp.cos(vertical * layer_thick)]
    all_to_all x1 -> x2, waiting for transfers between devices: 24.8 us -> 12.5 us  [shards(): lax.all_to_all(cross[:, None], 'freq', split_axis=2, concat_axis=1, tiled...]
    select_n x3 -> x1, other arithmetic: 9.39 us -> 1.19 us  [shards(): windows.append(jnp.where(slab // slab_count == freq_rank, window, 0))]
  transfers between devices with their start and end apart: 2 -> 2, of which waited for: 2 -> 1; matrix products, arithmetic and copies ran while one was open for 20% -> 2% of each run, Pallas kernels for 0% -> 15%
where the time goes in v1:
time: 123 us; the launch traced here: 121 us
  Pallas kernels  59.2 us (48%)
  local copies, waits for them, and re-layouts  19.9 us (16%)
  waiting for transfers between devices  12.5 us (10%)
  starting transfers between devices  11.9 us (10%)
  matrix products  8.55 us (7%)
  between operations  5.85 us (5%)
  other arithmetic  2.78 us (2%)
    pallas_call x2, Pallas kernels, depth_step(): pl.pallas_call(step_kernel, out_shape=(field, field, field), in_specs=[pl...  36.3 us
    pallas_call x1, Pallas kernels, share(): pl.pallas_call(functools.partial(share_kernel, devices), out_shape=jax.Sh...  22.9 us
    all_to_all x2, waiting for transfers between devices, shards(): lax.all_to_all(cross[:, None], 'freq', split_axis=2, concat_axis=1, tiled...  12.5 us
    all_to_all x2, starting transfers between devices, shards(): lax.all_to_all(cross[:, None], 'freq', split_axis=2, concat_axis=1, tiled...  11.9 us
    dot_general x1, matrix products, shards(): jnp.einsum('dcwab,cwl->dabl', jnp.stack(crosses), lag_weights, preferred_...  8.55 us
    unnamed x22, local copies, waits for them, and re-layouts  8.39 us
    broadcast_in_dim x2, local copies, waits for them, and re-layouts, shards(): cross[:, None]  2.66 us
  transfers between devices with their start and end apart: 2, of which 1 were waited for; matrix products, arithmetic and copies ran while one was open for 2% of the time, Pallas kernels for 15%

profile of v1, /device:TPU:9, one launch (start us, length us, event | category | flops | bytes accessed | tf_op | source)
XLA Modules:
  0.0 120.7 jit_solution(12424648723716075875)
XLA Ops:
  0.0 1.2 %dynamic_slice.10 = s32[1]{0:T(128)} dynamic-slice(s32[16]{0:T(128)} %param.16, s32[]{:T(128)S(6)} %select_n.57), dynamic_slice_sizes={1} | dynamic-slice | bytes 12 | tf_op jit(solution)/shard_map/jit(dynamic_index_in_dim)/dynamic_slice | solution.py:303
  1.9 1.3 %fusion.14 = (s32[1]{0:T(128)}, s32[1]{0:T(128)}) fusion(s32[2]{0:T(128)} %param.13), kind=kLoop, calls=%fused_computation.34 | loop fusion | bytes 16 | tf_op jit(solution)/shard_map/slice | solution.py:309
  5.8 1.3 %fusion.15 = (s32[1]{0:T(128)}, s32[1]{0:T(128)}) fusion(s32[2]{0:T(128)} %param.17), kind=kLoop, calls=%fused_computation.35 | loop fusion | bytes 16 | tf_op jit(solution)/shard_map/slice | solution.py:312
  10.9 1.2 broadcast_select_fusion.1
  12.1 0.8 pad_maximum_fusion.mine
  12.9 22.9 %shard_map.100 = bf16[2,8,64,256]{3,2,1,0:T(8,128)(2,1)} custom-call(bf16[2,8,64,256]{3,2,1,0:T(8,128)(2,1)} %pad_maximum_fusion.mine), custom_call_target="tpu_custom_call" | custom-call | tf_op jit(solution)/shard_map/pallas_call | solution.py:266
  35.9 1.1 fusion.13
  37.0 1.3 %slice_bitcast_fusion = (s32[512,256]{1,0:T(8,128)S(1)}, s32[512,256]{1,0:T(8,128)S(1)}) fusion(s32[2,512,256]{2,1,0:T(8,128)} %param.15), kind=kLoop, calls=%fused_computation.5 | loop fusion | bytes 2097152 | tf_op jit(solution)/shard_map/squeeze | solution.py:326
  38.3 1.0 copy-done
  39.4 1.0 copy-done.1
  40.4 1.6 %copy-done.2 = bf16[1024,1024]{1,0:T(8,128)(2,1)S(1)} copy-done((bf16[1024,1024]{1,0:T(8,128)(2,1)S(1)}, bf16[1024,1024]{1,0:T(8,128)(2,1)}, u32[]{:S(2)}) %copy-start.2) | copy-done | bytes 2097176
  42.0 1.0 copy-done.4
  43.1 17.6 %shard_map.101 = (bf16[2,512,256]{2,1,0:T(8,128)(2,1)S(1)}, bf16[2,512,256]{2,1,0:T(8,128)(2,1)S(1)}, bf16[2,512,256]{2,1,0:T(8,128)(2,1)S(1)}) custom-call(f32[6]{0:T(128)S(1)} %get-tuple-element.31.scalars, bf16[2,512,256]{2,1,0:T(8,128)(2,1)S(1)} %bitcast.42, bf16[2,512,256]{2,1,0:T(8,128)(2,1)S(1)} %bitcast.43, bf16[1024,1024]{1,0:T(8,128)(2,1)S(1)} %copy-done.2, ...), custom_call_target="tpu_custom_call" | custom-call | flops 19327352832 | bytes 8388608 | tf_op jit(solution)/shard_map/pallas_call | solution.py:180
  61.5 0.8 copy-done.8
  62.3 1.3 %copy.15 = bf16[2,1,512,256]{3,0,1,2:T(2,128)(2,1)} copy(bf16[2,1,512,256]{3,2,0,1:T(8,128)(2,1)S(1)} %bitcast.39) | data formatting | bytes 1048576 | tf_op jit(solution)/shard_map/broadcast_in_dim | solution.py:329
  63.6 5.9 %all-to-all-start = ((bf16[2,1,512,256]{3,0,1,2:T(2,128)(2,1)}), bf16[2,1,512,256]{3,0,1,2:T(2,128)(2,1)}, u32[]{:S(2)}, u32[]{:S(2)}) async-start(bf16[2,1,512,256]{3,0,1,2:T(2,128)(2,1)} %copy.15), calls=%async_computation | async-start | bytes 1048576 | tf_op jit(solution)/shard_map/all_to_all | solution.py:329
  69.6 1.0 copy-done.7
  70.6 1.0 copy-done.9
  71.6 18.6 %shard_map.102 = (bf16[2,512,256]{2,1,0:T(8,128)(2,1)}, bf16[2,512,256]{2,1,0:T(8,128)(2,1)}, bf16[2,512,256]{2,1,0:T(8,128)(2,1)S(1)}) custom-call(f32[6]{0:T(128)S(1)} %get-tuple-element.32.scalars, bf16[2,512,256]{2,1,0:T(8,128)(2,1)S(1)} %copy-done.7, bf16[2,512,256]{2,1,0:T(8,128)(2,1)S(1)} %copy-done.9, bf16[1024,1024]{1,0:T(8,128)(2,1)S(1)} %copy-done.3, ...), custom_call_target="tpu_custom_call" | custom-call | flops 19327352832 | bytes 8388608 | tf_op jit(solution)/shard_map/pallas_call | solution.py:180
  90.3 1.3 %copy.17 = bf16[2,1,512,256]{3,0,1,2:T(2,128)(2,1)} copy(bf16[2,1,512,256]{3,2,0,1:T(8,128)(2,1)S(1)} %bitcast.38) | data formatting | bytes 1048576 | tf_op jit(solution)/shard_map/broadcast_in_dim | solution.py:329
  91.6 6.0 %all-to-all-start.1 = ((bf16[2,1,512,256]{3,0,1,2:T(2,128)(2,1)}), bf16[2,1,512,256]{3,0,1,2:T(2,128)(2,1)S(1)}, u32[]{:S(2)}, u32[]{:S(2)}) async-start(bf16[2,1,512,256]{3,0,1,2:T(2,128)(2,1)} %copy.17), calls=%async_computation.1 | async-start | bytes 1048576 | tf_op jit(solution)/shard_map/all_to_all | solution.py:329
  97.8 1.5 %copy.19 = bf16[1,2,16,32,256]{4,2,1,3,0:T(8,128)(2,1)S(1)} copy(bf16[1,2,16,32,256]{4,1,3,2,0:T(2,128)(2,1)} %bitcast.14) | data formatting | bytes 1048576 | tf_op jit(solution)/shard_map/stack | solution.py:333
  99.3 12.5 %all-to-all-done.1 = bf16[2,1,512,256]{3,0,1,2:T(2,128)(2,1)S(1)} async-done(((bf16[2,1,512,256]{3,0,1,2:T(2,128)(2,1)}), bf16[2,1,512,256]{3,0,1,2:T(2,128)(2,1)S(1)}, u32[]{:S(2)}, u32[]{:S(2)}) %all-to-all-start.1) | async-done | bytes 524320 | tf_op jit(solution)/shard_map/all_to_all | solution.py:329
  112.2 8.5 %bitcast_multiply_fusion = f32[2,32,256,256]{3,2,1,0:T(8,128)} fusion(bf16[1,2,16,32,256]{4,2,1,3,0:T(8,128)(2,1)S(1)} %copy.20, bf16[1,2,16,32,256]{4,2,1,3,0:T(8,128)(2,1)S(1)} %copy.19, bf16[1,16,256]{2,1,0:T(8,128)(2,1)S(1)} %get-tuple-element.20, bf16[1,16,256]{2,1,0:T(8,128)(2,1)S(1)} %get-tuple-element.19), kind=kOutput, calls=%fused_computation | convolution fusion | flops 273162240 | bytes 17842176 | tf_op jit(solution)/shard_map/dcwab,cwl->dabl/dot_general | solution.py:332
  (27 shorter events, 2.8 us)
Async XLA Ops:
  38.3 1.0 copy-start
  39.4 1.0 copy-start.1
  40.4 1.6 %copy-start.2 = (bf16[1024,1024]{1,0:T(8,128)(2,1)S(1)}, bf16[1024,1024]{1,0:T(8,128)(2,1)}, u32[]{:S(2)}) copy-start(bf16[1024,1024]{1,0:T(8,128)(2,1)} %constant.80.clone.table_x) | copy-start | bytes 6291460
  42.0 1.0 copy-start.4
  43.1 26.5 %copy-start.3 = (bf16[1024,1024]{1,0:T(8,128)(2,1)S(1)}, bf16[1024,1024]{1,0:T(8,128)(2,1)}, u32[]{:S(2)}) copy-start(bf16[1024,1024]{1,0:T(8,128)(2,1)} %constant.80.clone.table_x) | copy-start | bytes 6291460
  43.1 26.5 %copy-start.5 = (bf16[512,512]{1,0:T(8,128)(2,1)S(1)}, bf16[512,512]{1,0:T(8,128)(2,1)}, u32[]{:S(2)}) copy-start(bf16[512,512]{1,0:T(8,128)(2,1)} %constant.81.clone.table_y) | copy-start | bytes 1572868
  60.7 0.8 copy-start.6
  61.5 0.8 copy-start.8
  63.6 28.0 %all-to-all-start = ((bf16[2,1,512,256]{3,0,1,2:T(2,128)(2,1)}), bf16[2,1,512,256]{3,0,1,2:T(2,128)(2,1)}, u32[]{:S(2)}, u32[]{:S(2)}) async-start(bf16[2,1,512,256]{3,0,1,2:T(2,128)(2,1)} %copy.15), calls=%async_computation | async-start | bytes 1048576 | tf_op jit(solution)/shard_map/all_to_all | solution.py:329
  69.6 1.0 copy-start.7
  70.6 1.0 copy-start.9
  71.6 26.0 %copy-start.10 = (s32[16]{0:T(128)S(1)}, s32[16]{0:T(128)}, u32[]{:S(2)}) copy-start(s32[16]{0:T(128)} %param.16) | copy-start | bytes 196
  91.6 20.1 %all-to-all-start.1 = ((bf16[2,1,512,256]{3,0,1,2:T(2,128)(2,1)}), bf16[2,1,512,256]{3,0,1,2:T(2,128)(2,1)S(1)}, u32[]{:S(2)}, u32[]{:S(2)}) async-start(bf16[2,1,512,256]{3,0,1,2:T(2,128)(2,1)} %copy.17), calls=%async_computation.1 | async-start | bytes 1048576 | tf_op jit(solution)/shard_map/all_to_all | solution.py:329

commit v2 on v0

v2 whole, which is shorter than its diff:
```python
import functools
import math

import jax
import jax.numpy as jnp
import numpy as np
from jax import lax
from jax.experimental import pallas as pl
from jax.experimental.pallas import tpu as pltpu
from jax.sharding import PartitionSpec as P

LAGS = 256

cell_width = 0.0125
layer_thick = 0.0125
bin_hertz = 0.5
period_bins = 500
slow_base = 0.3
chunk = 16
tile = 256


def spectral_order(length):
    half = length // 2
    return np.concatenate([np.arange(half), [half], np.arange(length - 1, half, -1)])


def parts_of(length):
    steps = np.arange(length, dtype=np.int64)
    phases = np.mod(steps[:, None] * steps[None, :], length).astype(np.float32)
    angles = phases * np.float32(2.0 * math.pi / length)
    scale = np.float32(1.0 / math.sqrt(length))
    return np.cos(angles) * scale, np.sin(angles) * scale


def transform_block(length):
    cosine, sine = parts_of(length)
    return np.block([[cosine, -sine], [sine, cosine]]).astype(jnp.bfloat16)


def transform_pair(length):
    cosine, sine = parts_of(length)
    order = spectral_order(length)
    return (
        np.concatenate([cosine[order], sine[order]], axis=1).astype(jnp.bfloat16),
        np.concatenate([cosine[:, order], sine[:, order]], axis=1).astype(jnp.bfloat16),
    )


def lag_table(frequency_bins, lag_count):
    offsets = jnp.arange(lag_count, dtype=jnp.int32) - lag_count // 2
    cycles = jnp.mod(frequency_bins[:, None] * offsets[None, :], period_bins).astype(jnp.float32)
    angles = cycles * (2.0 * math.pi / period_bins)
    return jnp.stack([jnp.cos(angles), -jnp.sin(angles)]).astype(jnp.bfloat16)


def sin_cos(angle):
    turns = jnp.floor(angle * (2.0 / math.pi) + 0.5)
    rest = angle - turns * 1.5707855224609375
    rest = rest - turns * 1.0804334124e-05
    quarter = turns.astype(jnp.int32)
    square = rest * rest
    sine = rest + rest * square * (
        -1.6666654611e-1 + square * (8.3321608736e-3 + square * -1.9515295891e-4)
    )
    cosine = (
        1.0
        - 0.5 * square
        + square * square
        * (4.166664568298827e-2 + square * (-1.388731625493765e-3 + square * 2.443315711809948e-5))
    )
    odd = (quarter & 1) == 1
    sine_out = jnp.where(odd, cosine, sine)
    cosine_out = jnp.where(odd, sine, cosine)
    sine_out = jnp.where((quarter & 2) == 2, -sine_out, sine_out)
    cosine_out = jnp.where(((quarter + 1) & 2) == 2, -cosine_out, cosine_out)
    return sine_out, cosine_out


def window_kernel(
    devices, scalars, source, receiver, table_f, table_i, table_y, windows, bracket,
    received,
    half, spectrum, shifted_a, shifted_b, returned, refocused, fields, cross,
    pair, part, parts, total, slow,
    pair_sems, scatter_sems, gather_sems, cross_sems,
):
    depths, rows_x, cols_y = bracket.shape
    chips = devices // 2
    me = lax.axis_index("freq")
    grp = lax.axis_index("grp")
    core = lax.rem(me, 2)
    chip = me // 2
    other = 1 - core
    share_rows = rows_x // devices
    signs = (1.0, -1.0)
    middle = rows_x // 2

    def lanes(which):
        return pl.ds(which * cols_y, cols_y)

    def remote(source_ref, target_ref, sems, place):
        return pltpu.make_async_remote_copy(
            src_ref=source_ref, dst_ref=target_ref, send_sem=sems[0], recv_sem=sems[1],
            device_id=(grp, place), device_id_type=pl.DeviceIdType.MESH,
        )

    def hop_to(hop):
        return lax.rem(chip + hop, chips)

    def swap_first(d):
        return remote(
            windows.at[d, other], pair.at[d], (pair_sems.at[d, 0], pair_sems.at[d, 1]),
            chip * 2 + other,
        )

    def scatter(d, hop):
        return remote(
            part.at[d, hop_to(hop)], parts.at[d, hop],
            (scatter_sems.at[d, 0, hop], scatter_sems.at[d, 1, hop]), hop_to(hop) * 2 + core,
        )

    def gather(d, hop):
        return remote(
            total.at[d], slow.at[d, core, chip],
            (gather_sems.at[d, 0, hop], gather_sems.at[d, 1, hop]), hop_to(hop) * 2 + core,
        )

    def swap_last(d):
        return remote(
            slow.at[d, core], slow.at[d, core], (pair_sems.at[d, 2], pair_sems.at[d, 3]),
            chip * 2 + other,
        )

    def send_cross(d, hop):
        to = lax.rem(me + hop, devices)
        return remote(
            cross.at[d, to], received.at[d, me],
            (cross_sems.at[d, 0, hop], cross_sems.at[d, 1, hop]), to,
        )

    def begin_scatter(d):
        swap_first(d).wait()
        part[d] = windows[d, core] + pair[d]

        @pl.loop(1, chips)
        def _(hop):
            scatter(d, hop).start()

    def begin_gather(d):
        @pl.loop(1, chips)
        def _(hop):
            scatter(d, hop).wait()

        summed = part[d, chip]
        for hop in range(1, chips):
            summed = summed + parts[d, hop]
        total[d] = summed
        slow[d, core, chip] = summed

        @pl.loop(1, chips)
        def _(hop):
            gather(d, hop).start()

    def begin_last(d):
        @pl.loop(1, chips)
        def _(hop):
            gather(d, hop).wait()

        swap_last(d).start()

    barrier = pltpu.get_barrier_semaphore()

    @pl.loop(1, devices)
    def _(hop):
        pl.semaphore_signal(
            barrier, inc=1, device_id=(grp, lax.rem(me + hop, devices)),
            device_id_type=pl.DeviceIdType.MESH,
        )

    pl.semaphore_wait(barrier, devices - 1)
    for d in range(depths):
        swap_first(d).start()

    columns = lax.broadcasted_iota(jnp.int32, (chunk, cols_y), 1)
    wave_y = jnp.where(columns < cols_y // 2, columns, cols_y - columns).astype(jnp.float32) * (
        2.0 * math.pi / (cols_y * cell_width)
    )
    squares_y = wave_y * wave_y

    def phases(d, ref, magnitude):
        wave_x = magnitude.astype(jnp.float32) * (2.0 * math.pi / (rows_x * cell_width))
        reach = scalars[d, 0] * scalars[d, 1 + ref]
        radicand = reach * reach - (wave_x * wave_x + squares_y)
        depth = jnp.sqrt(jnp.abs(radicand)) * layer_thick
        moving = radicand > 0.0
        fading = jnp.exp(jnp.where(moving, 0.0, -depth))
        sine, cosine = sin_cos(jnp.where(moving, depth, 0.0) - reach * layer_thick)
        return fading * cosine, fading * sine

    def apply_phase(target, cosine, sine, start):
        rows = pl.ds(start, chunk)
        low_rows = pl.ds(rows_x + start, chunk)
        for which in range(2):
            turned = signs[which] * sine
            real = spectrum[rows, lanes(which)]
            imag = spectrum[low_rows, lanes(which)]
            new_real = (cosine * real - turned * imag).astype(jnp.bfloat16)
            target[rows, lanes(which)] = new_real
            target[low_rows, lanes(which)] = (-(cosine * imag + turned * real)).astype(jnp.bfloat16)
            target[pl.ds(2 * rows_x + start, chunk), lanes(which)] = -new_real

    counted = lax.broadcasted_iota(jnp.int32, (chunk, cols_y), 0)

    def shift_chunk(d, ref, target, start):
        cosine, sine = phases(d, ref, counted + start)
        apply_phase(target, cosine, sine, start)
        apply_phase(target, cosine, sine, pl.multiple_of(middle + start, chunk))

    def shift_edge(d, ref, target):
        cosine, sine = phases(d, ref, jnp.where(counted == 0, middle, counted))
        apply_phase(target, cosine, sine, middle)

    def multiply(table, values, rows):
        block = table[rows, :]
        real = jnp.dot(block, values[: 2 * rows_x, :], preferred_element_type=jnp.float32)
        imag = jnp.dot(block, values[rows_x:, :], preferred_element_type=jnp.float32)
        return real, imag

    def slow_rows(d, start):
        if share_rows >= chunk:
            block = start // share_rows
            inner = pl.multiple_of(lax.rem(start, share_rows), chunk)
            return slow[d, block // chips, lax.rem(block, chips), pl.ds(inner, chunk), :].astype(
                jnp.float32
            )
        pieces = []
        for piece in range(chunk // share_rows):
            block = start // share_rows + piece
            pieces.append(
                slow[d, block // chips, lax.rem(block, chips)].astype(jnp.float32)
            )
        return jnp.concatenate(pieces, axis=0)

    def store_cross(d, start, which, values):
        if share_rows >= chunk:
            inner = pl.multiple_of(lax.rem(start, share_rows), chunk)
            cross[d, start // share_rows, which, pl.ds(inner, chunk), :] = values.astype(
                jnp.bfloat16
            )
        else:
            for piece in range(chunk // share_rows):
                cross[d, start // share_rows + piece, which] = values[
                    piece * share_rows : (piece + 1) * share_rows
                ].astype(jnp.bfloat16)

    for d in range(depths):
        for which, field in enumerate((source, receiver) if d == 0 else (fields.at[0], fields.at[1])):
            for start in range(0, rows_x, tile):
                rows = pl.ds(start, tile)
                both = jnp.concatenate([field[0, rows, :], field[1, rows, :]], axis=1)
                out = jnp.dot(both, table_y[...], preferred_element_type=jnp.float32)
                out = out.astype(jnp.bfloat16)
                half[rows, lanes(which)] = out[:, :cols_y]
                half[pl.ds(rows_x + start, tile), lanes(which)] = out[:, cols_y:]
                half[pl.ds(2 * rows_x + start, tile), lanes(which)] = -out[:, :cols_y]
        if d == 0:
            begin_scatter(0)

        @pl.loop(0, rows_x // tile)
        def _(number):
            start = pl.multiple_of(number * tile, tile)
            real, imag = multiply(table_f, half, pl.ds(start, tile))
            spectrum[pl.ds(start, tile), :] = real
            spectrum[pl.ds(rows_x + start, tile), :] = imag

        if d == 0:
            begin_gather(0)
            for later in range(1, depths):
                begin_scatter(later)

        @pl.loop(0, middle // chunk)
        def _(number):
            shift_chunk(d, 0, shifted_a, pl.multiple_of(number * chunk, chunk))

        shift_edge(d, 0, shifted_a)
        for ref in range(3):
            now, later_shift = (shifted_a, shifted_b) if ref % 2 == 0 else (shifted_b, shifted_a)
            per_tile = middle // chunk // (rows_x // tile)

            @pl.loop(0, rows_x // tile)
            def _(number):
                start = pl.multiple_of(number * tile, tile)
                real, imag = multiply(table_i, now, pl.ds(start, tile))
                returned[pl.ds(start, tile), :] = real.astype(jnp.bfloat16)
                returned[pl.ds(rows_x + start, tile), :] = imag.astype(jnp.bfloat16)
                if ref < 2:
                    for each in range(per_tile):
                        shift_chunk(
                            d, ref + 1, later_shift,
                            pl.multiple_of((number * per_tile + each) * chunk, chunk),
                        )

            if ref < 2:
                shift_edge(d, ref + 1, later_shift)
            for which in range(2):
                for start in range(0, rows_x, tile):
                    rows = pl.ds(start, tile)
                    both = jnp.concatenate(
                        [
                            returned[rows, lanes(which)],
                            returned[pl.ds(rows_x + start, tile), lanes(which)],
                        ],
                        axis=1,
                    )
                    refocused[ref, which, rows, :] = jnp.dot(
                        both, table_y[...], preferred_element_type=jnp.float32
                    )
            if d == 0 and ref == 0:
                begin_last(0)
                for later in range(1, depths):
                    begin_gather(later)
            if d == 0 and ref == 1:
                for later in range(1, depths):
                    begin_last(later)
        if d == 0:
            for each in range(depths):
                swap_last(each).wait()

        @pl.loop(0, rows_x // chunk)
        def _(number):
            start = pl.multiple_of(number * chunk, chunk)
            rows = pl.ds(start, chunk)
            slowness = slow_rows(d, start)
            lower = bracket[d, rows, :] == 0
            slow_low = jnp.where(lower, scalars[d, 1], scalars[d, 2])
            slow_gap = jnp.where(lower, scalars[d, 4], scalars[d, 5])
            weight = jnp.clip((slowness - slow_low) / slow_gap, 0.0, 1.0)
            sine, cosine = sin_cos((scalars[d, 0] * layer_thick) * slowness)
            rounded = []
            for which in range(2):
                mixed = []
                for side in range(2):
                    first = refocused[0, which, rows, lanes(side)]
                    second = refocused[1, which, rows, lanes(side)]
                    third = refocused[2, which, rows, lanes(side)]
                    low = jnp.where(lower, first, second)
                    high = jnp.where(lower, second, third)
                    mixed.append((1.0 - weight) * low + weight * high)
                turned = signs[which] * sine
                real = (cosine * mixed[0] + turned * mixed[1]).astype(jnp.bfloat16)
                imag = (turned * mixed[0] - cosine * mixed[1]).astype(jnp.bfloat16)
                if d < depths - 1:
                    fields[which, 0, rows, :] = real
                    fields[which, 1, rows, :] = imag
                rounded.append((real.astype(jnp.float32), imag.astype(jnp.float32)))
            (sr, si), (rr, ri) = rounded
            store_cross(d, start, 0, sr * rr + si * ri)
            store_cross(d, start, 1, sr * ri - si * rr)

        @pl.loop(1, devices)
        def _(hop):
            send_cross(d, hop).start()

        received[d, me] = cross[d, me]
    for d in range(depths):
        @pl.loop(1, devices)
        def _(hop):
            send_cross(d, hop).wait()


def cross_spectra(devices, scalars, source, receiver, windows, bracket):
    depths, rows_x, cols_y = bracket.shape
    chips = devices // 2
    share_rows = rows_x // devices
    table_f, table_i = transform_pair(rows_x)
    vmem = pl.BlockSpec(memory_space=pltpu.VMEM)
    flops = 16 * rows_x * (2 * rows_x + 2 * cols_y) * 2 * cols_y * depths
    dma = pltpu.SemaphoreType.DMA
    held = (depths, chips, share_rows, cols_y)
    return pl.pallas_call(
        functools.partial(window_kernel, devices),
        out_shape=jax.ShapeDtypeStruct((depths, devices, 2, share_rows, cols_y), jnp.bfloat16),
        in_specs=[pl.BlockSpec(memory_space=pltpu.SMEM)] + [vmem] * 7,
        out_specs=vmem,
        scratch_shapes=[
            pltpu.VMEM((3 * rows_x, 2 * cols_y), jnp.bfloat16),
            pltpu.VMEM((2 * rows_x, 2 * cols_y), jnp.float32),
            pltpu.VMEM((3 * rows_x, 2 * cols_y), jnp.bfloat16),
            pltpu.VMEM((3 * rows_x, 2 * cols_y), jnp.bfloat16),
            pltpu.VMEM((2 * rows_x, 2 * cols_y), jnp.bfloat16),
            pltpu.VMEM((3, 2, rows_x, 2 * cols_y), jnp.float32),
            pltpu.VMEM((2, 2, rows_x, cols_y), jnp.bfloat16),
            pltpu.VMEM((depths, devices, 2, share_rows, cols_y), jnp.bfloat16),
            pltpu.VMEM(held, jnp.bfloat16),
            pltpu.VMEM(held, jnp.bfloat16),
            pltpu.VMEM(held, jnp.bfloat16),
            pltpu.VMEM((depths, share_rows, cols_y), jnp.bfloat16),
            pltpu.VMEM((depths, 2, chips, share_rows, cols_y), jnp.bfloat16),
            dma((depths, 4)),
            dma((depths, 2, chips)),
            dma((depths, 2, chips)),
            dma((depths, 2, devices)),
        ],
        cost_estimate=pl.CostEstimate(
            flops=4 * flops, bytes_accessed=8 * 1024 * 1024, transcendentals=0
        ),
        compiler_params=pltpu.CompilerParams(
            collective_id=0, has_side_effects=True, vmem_limit_bytes=56 * 1024 * 1024
        ),
    )(
        scalars, source, receiver, jnp.asarray(table_f), jnp.asarray(table_i),
        jnp.asarray(transform_block(cols_y)),
        windows.reshape(depths, 2, chips, share_rows, cols_y), bracket,
    )


def shards(
    devices,
    source_field,
    receiver_field,
    slowness_slabs,
    slab_map,
    reference_gaps,
    reference_index,
    frequency_bins,
    shot_corner,
):
    rows_x = source_field.shape[2]
    cols_y = source_field.shape[3]
    depths = slab_map.shape[0]
    freq_rank = lax.axis_index("freq")
    slab_count = slowness_slabs.shape[0]
    angular = lax.dynamic_index_in_dim(frequency_bins, freq_rank, 0, False).astype(
        jnp.float32
    ) * (2.0 * math.pi * bin_hertz)
    lag_weights = lag_table(frequency_bins, LAGS)
    windows = []
    for depth in range(depths):
        slab = slab_map[depth]
        window = lax.dynamic_slice(
            slowness_slabs,
            (slab % slab_count, shot_corner[0], shot_corner[1]),
            (1, rows_x, cols_y),
        )[0]
        windows.append(jnp.where(slab // slab_count == freq_rank, window, 0))
    references = slow_base + jnp.cumsum(reference_gaps, axis=1)
    scalars = jnp.concatenate(
        [
            jnp.broadcast_to(angular, (depths, 1)),
            references,
            references[:, 1:] - references[:, :-1],
        ],
        axis=1,
    )
    crosses = cross_spectra(
        devices, scalars, source_field[:, 0], receiver_field[:, 0], jnp.stack(windows),
        reference_index,
    )
    scale = frequency_bins.shape[0] ** (-0.5)
    return (
        jnp.einsum(
            "dwcab,cwl->dabl", crosses, lag_weights, preferred_element_type=jnp.float32
        )
        * scale
    )


def solution(mesh):
    placed = (
        P("grp", "freq", None, None),
        P("grp", "freq", None, None),
        P(("grp", "freq"), None, None),
        P("grp"),
        P("grp", None),
        P("grp", None, None),
        P(),
        P("grp"),
    )
    return jax.shard_map(
        functools.partial(shards, mesh.shape["freq"]),
        mesh=mesh,
        in_specs=placed,
        out_specs=P("grp", "freq", None, None),
        check_vma=False,
    )
```

time: 222 us -> 80.5 us (0.36)
  waiting for transfers between devices: 71 us -> 0 us
  other arithmetic: 72.8 us -> 4.42 us
  Pallas kernels: 0 us -> 56 us
  matrix products: 35.3 us -> 9.82 us
  between operations: 19.5 us -> 5.82 us
  local copies, waits for them, and re-layouts: 16.4 us -> 3.89 us
  starting transfers between devices: 6.48 us -> 0 us
    pallas_call x0 -> x1, Pallas kernels: none -> 56 us  [cross_spectra(): pl.pallas_call(functools.partial(window_kernel, devices), out_shape=jax.S...]
    psum x1 -> x0, waiting for transfers between devices: 46.2 us -> none  [spread(): return lax.psum(block, axis)]
    dot_general x6 -> x1, matrix products: 35.3 us -> 9.82 us  [shards(): jnp.einsum('dwcab,cwl->dabl', crosses, lag_weights, preferred_element_typ...]
    all_to_all x1 -> x0, waiting for transfers between devices: 24.8 us -> none  [shards(): lax.all_to_all(all_crosses, 'freq', split_axis=3, concat_axis=2, tiled=True)]
    another operation x15 -> x3, other arithmetic: 25.4 us -> 2.5 us  [the longest x1 0.85 us: shards(): references = slow_base + jnp.cumsum(reference_gaps, axis=1)]
    sub x3 -> x1, other arithmetic: 17.6 us -> 0.08 us  [shards(): references[:, 1:] - references[:, :-1]]
    mul x2 -> x0, other arithmetic: 14.4 us -> none  [the longest x1 14.4 us: phase_factors(): fading * jnp.cos(vertical * layer_thick)]
    select_n x3 -> x1, other arithmetic: 9.39 us -> 1.19 us  [shards(): windows.append(jnp.where(slab // slab_count == freq_rank, window, 0))]
  transfers between devices with their start and end apart: 2 -> 0, of which waited for: 2 -> 0; matrix products, arithmetic and copies ran while one was open for 20% -> 0% of each run, Pallas kernels for 0% -> 0%
where the time goes in v2:
time: 80.5 us; the launch traced here: 80 us
  Pallas kernels  56 us (70%)
  matrix products  9.82 us (12%)
  between operations  5.82 us (7%)
  other arithmetic  4.42 us (5%)
  local copies, waits for them, and re-layouts  3.89 us (5%)
    pallas_call x1, Pallas kernels, cross_spectra(): pl.pallas_call(functools.partial(window_kernel, devices), out_shape=jax.S...  56 us
    dot_general x1, matrix products, shards(): jnp.einsum('dwcab,cwl->dabl', crosses, lag_weights, preferred_element_typ...  9.82 us

profile of v2, /device:TPU:9, one launch (start us, length us, event | category | flops | bytes accessed | tf_op | source)
XLA Modules:
  0.0 80.0 jit_solution(2029496788909230700)
XLA Ops:
  0.0 1.2 %dynamic_slice.10 = s32[1]{0:T(128)} dynamic-slice(s32[16]{0:T(128)} %param.17, s32[]{:T(128)S(6)} %select_n.57), dynamic_slice_sizes={1} | dynamic-slice | bytes 12 | tf_op jit(solution)/shard_map/jit(dynamic_index_in_dim)/dynamic_slice | solution.py:433
  1.9 0.9 %reduce_window_sum.11 = f32[2,3]{1,0:T(2,128)S(1)} reduce-window(f32[2,3]{1,0:T(2,128)} %param.15, f32[]{:T(128)} %constant.72.clone.1), window={size=1x3 pad=0_0x2_0}, to_apply=%region_0.1 | reduce-window | flops 12 | bytes 52 | tf_op jit(solution)/shard_map/jit(cumsum)/reduce_window_sum | solution.py:446
  2.8 0.1 slice_subtract_fusion
  2.8 0.6 pad_maximum_fusion.1.scalars
  3.5 1.3 %fusion.9 = (s32[1]{0:T(128)}, s32[1]{0:T(128)}) fusion(s32[2]{0:T(128)} %param.14), kind=kLoop, calls=%fused_computation.22 | loop fusion | bytes 16 | tf_op jit(solution)/shard_map/slice | solution.py:439
  6.1 1.3 %fusion.10 = (s32[1]{0:T(128)}, s32[1]{0:T(128)}) fusion(s32[2]{0:T(128)} %param.18), kind=kLoop, calls=%fused_computation.23 | loop fusion | bytes 16 | tf_op jit(solution)/shard_map/slice | solution.py:442
  11.3 0.8 %cosine_convert_fusion = (bf16[1,16,256]{2,1,0:T(8,128)(2,1)S(1)}, bf16[1,16,256]{2,1,0:T(8,128)(2,1)S(1)}) fusion(s32[256]{0:T(256)S(1)} %iota_add_fusion, s32[16]{0:T(128)} %param.17), kind=kLoop, calls=%fused_computation.12 | loop fusion | flops 49152 | bytes 17472 | tf_op jit(solution)/shard_map/convert
  12.1 1.2 %broadcast_select_fusion.1 = (bf16[1,512,256]{2,1,0:T(8,128)(2,1)S(1)}, bf16[1,512,256]{2,1,0:T(8,128)(2,1)S(1)}) fusion(pred[]{:T(512)S(6)} %eq.11, bf16[1,768,512]{2,1,0:T(8,128)(2,1)} %param.13, s32[]{:T(128)S(6)} %select_n.59, s32[]{:T(128)S(6)} %select_n.60, pred[]{:T(512)S(6)} %eq.12), kind=kLoop, calls=%fused_computation.4 | loop fusion | flops 262144 | bytes 786442 | tf_op jit(solution)/shard_map/jit(_where)/select_n | solution.py:445
  13.3 0.8 %pad_maximum_fusion.windows = bf16[2,2,8,32,256]{4,3,2,1,0:T(8,128)(2,1)} fusion(bf16[1,2,8,32,256]{4,3,2,1,0:T(8,128)(2,1)S(1)} %bitcast.18, bf16[1,2,8,32,256]{4,3,2,1,0:T(8,128)(2,1)S(1)} %bitcast.17), kind=kLoop, calls=%fused_computation.2 | loop fusion | flops 262144 | bytes 1048576 | tf_op jit(solution)/shard_map/stack | solution.py:456
  14.1 56.0 %shard_map.109 = bf16[2,16,2,32,256]{4,3,2,1,0:T(8,128)(2,1)} custom-call(f32[2,6]{1,0:T(2,128)} %pad_maximum_fusion.1.scalars, bf16[2,512,256]{2,1,0:T(8,128)(2,1)} %bitcast.19, bf16[2,512,256]{2,1,0:T(8,128)(2,1)} %bitcast.20, bf16[512,1024]{1,0:T(8,128)(2,1)} %constant.81.clone.table_f, bf16[512,1024]{1,0:T(8,128)(2,1)} %constant.82.clone.table_i, ...), custom_call_target="tpu_custom_call" | custom-call | flops 51539607552 | bytes 8388608 | tf_op jit(solution)/shard_map/pallas_call | solution.py:380
  70.2 9.8 %bitcast_multiply_fusion = f32[2,32,256,256]{3,2,1,0:T(8,128)} fusion(bf16[2,16,2,32,256]{4,3,2,1,0:T(8,128)(2,1)} %shard_map.109, bf16[1,16,256]{2,1,0:T(8,128)(2,1)S(1)} %get-tuple-element.8, bf16[1,16,256]{2,1,0:T(8,128)(2,1)S(1)} %get-tuple-element.7), kind=kOutput, calls=%fused_computation | convolution fusion | flops 272637952 | bytes 17842176 | tf_op jit(solution)/shard_map/dwcab,cwl->dabl/dot_general | solution.py:461
  (3 shorter events, 0.0 us)

commit v3 on v2

--- a/solution.py
+++ b/solution.py
@@ -78,7 +78,7 @@
 
 
 def window_kernel(
-    devices, scalars, source, receiver, table_f, table_i, table_y, windows, bracket,
+    devices, bins, gaps, source, receiver, table_f, table_i, table_y, windows, bracket,
     received,
     half, spectrum, shifted_a, shifted_b, returned, refocused, fields, cross,
     pair, part, parts, total, slow,
@@ -94,6 +94,13 @@
     share_rows = rows_x // devices
     signs = (1.0, -1.0)
     middle = rows_x // 2
+    angular = bins[me].astype(jnp.float32) * (2.0 * math.pi * bin_hertz)
+    references = []
+    for d in range(depths):
+        first = gaps[d, 0]
+        second = first + gaps[d, 1]
+        third = second + gaps[d, 2]
+        references.append((slow_base + first, slow_base + second, slow_base + third))
 
     def lanes(which):
         return pl.ds(which * cols_y, cols_y)
@@ -189,7 +196,7 @@
 
     def phases(d, ref, magnitude):
         wave_x = magnitude.astype(jnp.float32) * (2.0 * math.pi / (rows_x * cell_width))
-        reach = scalars[d, 0] * scalars[d, 1 + ref]
+        reach = angular * references[d][ref]
         radicand = reach * reach - (wave_x * wave_x + squares_y)
         depth = jnp.sqrt(jnp.abs(radicand)) * layer_thick
         moving = radicand > 0.0
@@ -332,10 +339,12 @@
             rows = pl.ds(start, chunk)
             slowness = slow_rows(d, start)
             lower = bracket[d, rows, :] == 0
-            slow_low = jnp.where(lower, scalars[d, 1], scalars[d, 2])
-            slow_gap = jnp.where(lower, scalars[d, 4], scalars[d, 5])
+            slow_low = jnp.where(lower, references[d][0], references[d][1])
+            slow_gap = jnp.where(
+                lower, references[d][1] - references[d][0], references[d][2] - references[d][1]
+            )
             weight = jnp.clip((slowness - slow_low) / slow_gap, 0.0, 1.0)
-            sine, cosine = sin_cos((scalars[d, 0] * layer_thick) * slowness)
+            sine, cosine = sin_cos((angular * layer_thick) * slowness)
             rounded = []
             for which in range(2):
                 mixed = []
@@ -368,7 +377,7 @@
             send_cross(d, hop).wait()
 
 
-def cross_spectra(devices, scalars, source, receiver, windows, bracket):
+def cross_spectra(devices, bins, gaps, source, receiver, windows, bracket):
     depths, rows_x, cols_y = bracket.shape
     chips = devices // 2
     share_rows = rows_x // devices
@@ -380,7 +389,7 @@
     return pl.pallas_call(
         functools.partial(window_kernel, devices),
         out_shape=jax.ShapeDtypeStruct((depths, devices, 2, share_rows, cols_y), jnp.bfloat16),
-        in_specs=[pl.BlockSpec(memory_space=pltpu.SMEM)] + [vmem] * 7,
+        in_specs=[pl.BlockSpec(memory_space=pltpu.SMEM)] * 2 + [vmem] * 7,
         out_specs=vmem,
         scratch_shapes=[
             pltpu.VMEM((3 * rows_x, 2 * cols_y), jnp.bfloat16),
@@ -408,10 +417,85 @@
             collective_id=0, has_side_effects=True, vmem_limit_bytes=56 * 1024 * 1024
         ),
     )(
-        scalars, source, receiver, jnp.asarray(table_f), jnp.asarray(table_i),
+        bins, gaps, source, receiver, jnp.asarray(table_f), jnp.asarray(table_i),
         jnp.asarray(transform_block(cols_y)),
         windows.reshape(depths, 2, chips, share_rows, cols_y), bracket,
     )
+
+
+def cut_kernel(slab_count, slab_map, corner, slab, out):
+    owner = slab_map[pl.program_id(0)] // slab_count
+    _, rows_x, cols_y = out.shape
+    _, rows_all, cols_all = slab.shape
+    held = lax.axis_index("freq")
+
+    @pl.when(owner != held)
+    def _():
+        out[...] = jnp.zeros(out.shape, out.dtype)
+
+    @pl.when(owner == held)
+    def _():
+        base = corner[0] // chunk * chunk
+        up = lax.rem(2 * chunk - (corner[0] - base), 2 * chunk)
+        left = lax.rem(cols_all - corner[1], cols_all)
+
+        @pl.loop(0, rows_x // chunk)
+        def _(number):
+            start = pl.multiple_of(base + number * chunk, chunk)
+            after = pl.multiple_of(jnp.minimum(start + chunk, rows_all - chunk), chunk)
+            both = jnp.concatenate(
+                [slab[0, pl.ds(start, chunk), :], slab[0, pl.ds(after, chunk), :]], axis=0
+            ).astype(jnp.float32)
+            both = pltpu.roll(both, up, 0)[:chunk]
+            both = pltpu.roll(both, left, 1)[:, :cols_y]
+            out[0, pl.ds(pl.multiple_of(number * chunk, chunk), chunk), :] = both.astype(out.dtype)
+
+
+def cut_windows(slab_map, corner, slabs, rows_x, cols_y):
+    slab_count, rows_all, cols_all = slabs.shape
+    depths = slab_map.shape[0]
+    return pl.pallas_call(
+        functools.partial(cut_kernel, slab_count),
+        out_shape=jax.ShapeDtypeStruct((depths, rows_x, cols_y), slabs.dtype),
+        grid_spec=pltpu.PrefetchScalarGridSpec(
+            num_scalar_prefetch=2,
+            grid=(depths,),
+            in_specs=[
+                pl.BlockSpec(
+                    (1, rows_all, cols_all),
+                    lambda d, slab_map, corner: (lax.rem(slab_map[d], slab_count), 0, 0),
+                )
+            ],
+            out_specs=pl.BlockSpec((1, rows_x, cols_y), lambda d, slab_map, corner: (d, 0, 0)),
+        ),
+    )(slab_map, corner, slabs)
+
+
+def image_kernel(scale, crosses, weights, out):
+    _, slots, _, rows, cols_y = crosses.shape
+    values = crosses[0].astype(jnp.float32).reshape(2 * slots, rows, cols_y)
+    values = jnp.swapaxes(values, 0, 1).astype(jnp.bfloat16)
+    for row in range(rows):
+        out[0, row] = scale * lax.dot_general(
+            values[row], weights[...], (((0,), (0,)), ((), ())),
+            preferred_element_type=jnp.float32,
+        )
+
+
+def lag_image(crosses, weights):
+    depths, slots, _, rows, cols_y = crosses.shape
+    lag_count = weights.shape[1]
+    step = min(8, rows)
+    return pl.pallas_call(
+        functools.partial(image_kernel, slots ** (-0.5)),
+        out_shape=jax.ShapeDtypeStruct((depths, rows, cols_y, lag_count), jnp.float32),
+        grid=(depths, rows // step),
+        in_specs=[
+            pl.BlockSpec((1, slots, 2, step, cols_y), lambda d, r: (d, 0, 0, r, 0)),
+            pl.BlockSpec((2 * slots, lag_count), lambda d, r: (0, 0)),
+        ],
+        out_specs=pl.BlockSpec((1, step, cols_y, lag_count), lambda d, r: (d, r, 0, 0)),
+    )(crosses, weights)
 
 
 def shards(
@@ -425,44 +509,14 @@
     frequency_bins,
     shot_corner,
 ):
-    rows_x = source_field.shape[2]
-    cols_y = source_field.shape[3]
-    depths = slab_map.shape[0]
-    freq_rank = lax.axis_index("freq")
-    slab_count = slowness_slabs.shape[0]
-    angular = lax.dynamic_index_in_dim(frequency_bins, freq_rank, 0, False).astype(
-        jnp.float32
-    ) * (2.0 * math.pi * bin_hertz)
-    lag_weights = lag_table(frequency_bins, LAGS)
-    windows = []
-    for depth in range(depths):
-        slab = slab_map[depth]
-        window = lax.dynamic_slice(
-            slowness_slabs,
-            (slab % slab_count, shot_corner[0], shot_corner[1]),
-            (1, rows_x, cols_y),
-        )[0]
-        windows.append(jnp.where(slab // slab_count == freq_rank, window, 0))
-    references = slow_base + jnp.cumsum(reference_gaps, axis=1)
-    scalars = jnp.concatenate(
-        [
-            jnp.broadcast_to(angular, (depths, 1)),
-            references,
-            references[:, 1:] - references[:, :-1],
-        ],
-        axis=1,
-    )
+    rows_x, cols_y = source_field.shape[2:]
+    lag_weights = jnp.swapaxes(lag_table(frequency_bins, LAGS), 0, 1)
+    windows = cut_windows(slab_map, shot_corner, slowness_slabs, rows_x, cols_y)
     crosses = cross_spectra(
-        devices, scalars, source_field[:, 0], receiver_field[:, 0], jnp.stack(windows),
-        reference_index,
-    )
-    scale = frequency_bins.shape[0] ** (-0.5)
-    return (
-        jnp.einsum(
-            "dwcab,cwl->dabl", crosses, lag_weights, preferred_element_type=jnp.float32
-        )
-        * scale
-    )
+        devices, frequency_bins, reference_gaps, source_field[:, 0], receiver_field[:, 0],
+        windows, reference_index,
+    )
+    return lag_image(crosses, lag_weights.reshape(-1, LAGS))
 
 
 def solution(mesh):

time: 80.5 us -> 72.3 us (0.90); the launches traced: 80 us -> 72.8 us
  Pallas kernels: 56 us -> 71.4 us
  matrix products: 9.82 us -> 0 us
  between operations: 5.82 us -> 0.03 us
  other arithmetic: 4.42 us -> 0.81 us
  local copies, waits for them, and re-layouts: 3.89 us -> 0.62 us
    pallas_call x0 -> x2, Pallas kernels: none -> 11.8 us  [the longest x1 9.2 us: lag_image(): pl.pallas_call(functools.partial(image_kernel, slots ** (-0.5)), out_shap...]
    dot_general x1 -> x0, matrix products: 9.82 us -> none  [shards(): jnp.einsum('dwcab,cwl->dabl', crosses, lag_weights, preferred_element_typ...]
    pallas_call x1, Pallas kernels: 56 us -> 59.5 us  [cross_spectra(): pl.pallas_call(functools.partial(window_kernel, devices), out_shape=jax.S...]
    slice x2 -> x0, local copies, waits for them, and re-layouts: 2.65 us -> none  [the longest x1 1.34 us: shards(): slab = slab_map[depth]]
    another operation x3 -> x1, other arithmetic: 2.5 us -> 0.81 us  [the longest x1 0.85 us: shards(): references = slow_base + jnp.cumsum(reference_gaps, axis=1)]
    dynamic_slice x1 -> x0, local copies, waits for them, and re-layouts: 1.24 us -> none  [shards(): lax.dynamic_index_in_dim(frequency_bins, freq_rank, 0, False)]
    select_n x1 -> x0, other arithmetic: 1.19 us -> none  [shards(): windows.append(jnp.where(slab // slab_count == freq_rank, window, 0))]
where the time goes in v3:
time: 72.3 us; the launch traced here: 72.8 us
  Pallas kernels  71.4 us (99%)
  other arithmetic  0.81 us (1%)
    pallas_call x1, Pallas kernels, cross_spectra(): pl.pallas_call(functools.partial(window_kernel, devices), out_shape=jax.S...  59.5 us
    pallas_call x1, Pallas kernels, lag_image(): pl.pallas_call(functools.partial(image_kernel, slots ** (-0.5)), out_shap...  9.2 us
    pallas_call x1, Pallas kernels, cut_windows(): pl.pallas_call(functools.partial(cut_kernel, slab_count), out_shape=jax.S...  2.64 us

profile of v3, /device:TPU:9, one launch (start us, length us, event | category | flops | bytes accessed | tf_op | source)
XLA Modules:
  0.0 72.8 jit_solution(2892654160427331014)
XLA Ops:
  0.0 0.8 %cosine_convert_fusion = (bf16[1,16,256]{2,1,0:T(8,128)(2,1)S(1)}, bf16[1,16,256]{2,1,0:T(8,128)(2,1)S(1)}) fusion(s32[256]{0:T(256)S(1)} %iota_add_fusion, s32[16]{0:T(128)} %bins.1), kind=kLoop, calls=%fused_computation.5 | loop fusion | flops 49152 | bytes 17472 | tf_op jit(solution)/shard_map/convert
  0.8 0.6 reshape.123.weights
  1.5 2.6 %shard_map.109 = bf16[2,512,256]{2,1,0:T(8,128)(2,1)} custom-call(s32[2]{0:T(128)} %slab_map.1, s32[2]{0:T(128)} %corner.1, bf16[1,768,512]{2,1,0:T(8,128)(2,1)} %slab.1), custom_call_target="tpu_custom_call" | custom-call | tf_op jit(solution)/shard_map/pallas_call | solution.py:457
  4.1 59.5 %shard_map.110.crosses = bf16[2,16,2,32,256]{4,3,2,1,0:T(8,128)(2,1)} custom-call(s32[16]{0:T(128)} %bins.1, f32[2,3]{1,0:T(2,128)} %gaps.1, bf16[2,512,256]{2,1,0:T(8,128)(2,1)} %bitcast.6, bf16[2,512,256]{2,1,0:T(8,128)(2,1)} %bitcast.7, bf16[512,1024]{1,0:T(8,128)(2,1)} %constant.23.clone.table_f, bf16[512,1024]{1,0:T(8,128)(2,1)} %constant.24.clone.table_i, ...), custom_call_target="tpu_custom_call" | custom-call | flops 51539607552 | bytes 8388608 | tf_op jit(solution)/shard_map/pallas_call | solution.py:389
  63.6 9.2 %shard_map.111 = f32[2,32,256,256]{3,2,1,0:T(8,128)} custom-call(bf16[2,16,2,32,256]{4,3,2,1,0:T(8,128)(2,1)} %shard_map.110.crosses, bf16[32,256]{1,0:T(8,128)(2,1)} %reshape.123.weights), custom_call_target="tpu_custom_call" | custom-call | tf_op jit(solution)/shard_map/pallas_call | solution.py:489
  (3 shorter events, 0.0 us)

commit v4 on v3

--- a/solution.py
+++ b/solution.py
@@ -80,7 +80,7 @@
 def window_kernel(
     devices, bins, gaps, source, receiver, table_f, table_i, table_y, windows, bracket,
     received,
-    half, spectrum, shifted_a, shifted_b, returned, refocused, fields, cross,
+    half, spectrum, shifted_a, shifted_b, shifted_c, returned, refocused, fields, cross,
     pair, part, parts, total, slow,
     pair_sems, scatter_sems, gather_sems, cross_sems,
 ):
@@ -94,6 +94,10 @@
     share_rows = rows_x // devices
     signs = (1.0, -1.0)
     middle = rows_x // 2
+    tiles = rows_x // tile
+    group = max(share_rows, chunk)
+    groups = tile // group
+    shifted = (shifted_a, shifted_b, shifted_c)
     angular = bins[me].astype(jnp.float32) * (2.0 * math.pi * bin_hertz)
     references = []
     for d in range(depths):
@@ -260,6 +264,38 @@
                     piece * share_rows : (piece + 1) * share_rows
                 ].astype(jnp.bfloat16)
 
+    def mix(d, inside, start):
+        local = pl.ds(inside, chunk)
+        rows = pl.ds(start, chunk)
+        slowness = slow_rows(d, start)
+        lower = bracket[d, rows, :] == 0
+        slow_low = jnp.where(lower, references[d][0], references[d][1])
+        slow_gap = jnp.where(
+            lower, references[d][1] - references[d][0], references[d][2] - references[d][1]
+        )
+        weight = jnp.clip((slowness - slow_low) / slow_gap, 0.0, 1.0)
+        sine, cosine = sin_cos((angular * layer_thick) * slowness)
+        rounded = []
+        for which in range(2):
+            mixed = []
+            for side in range(2):
+                first = refocused[0, which, local, lanes(side)]
+                second = refocused[1, which, local, lanes(side)]
+                third = refocused[2, which, local, lanes(side)]
+                low = jnp.where(lower, first, second)
+                high = jnp.where(lower, second, third)
+                mixed.append((1.0 - weight) * low + weight * high)
+            turned = signs[which] * sine
+            real = (cosine * mixed[0] + turned * mixed[1]).astype(jnp.bfloat16)
+            imag = (turned * mixed[0] - cosine * mixed[1]).astype(jnp.bfloat16)
+            if d < depths - 1:
+                fields[which, 0, rows, :] = real
+                fields[which, 1, rows, :] = imag
+            rounded.append((real.astype(jnp.float32), imag.astype(jnp.float32)))
+        (sr, si), (rr, ri) = rounded
+        store_cross(d, start, 0, sr * rr + si * ri)
+        store_cross(d, start, 1, sr * ri - si * rr)
+
     for d in range(depths):
         for which, field in enumerate((source, receiver) if d == 0 else (fields.at[0], fields.at[1])):
             for start in range(0, rows_x, tile):
@@ -287,89 +323,81 @@
 
         @pl.loop(0, middle // chunk)
         def _(number):
-            shift_chunk(d, 0, shifted_a, pl.multiple_of(number * chunk, chunk))
-
-        shift_edge(d, 0, shifted_a)
-        for ref in range(3):
-            now, later_shift = (shifted_a, shifted_b) if ref % 2 == 0 else (shifted_b, shifted_a)
-            per_tile = middle // chunk // (rows_x // tile)
-
-            @pl.loop(0, rows_x // tile)
-            def _(number):
-                start = pl.multiple_of(number * tile, tile)
-                real, imag = multiply(table_i, now, pl.ds(start, tile))
-                returned[pl.ds(start, tile), :] = real.astype(jnp.bfloat16)
-                returned[pl.ds(rows_x + start, tile), :] = imag.astype(jnp.bfloat16)
-                if ref < 2:
-                    for each in range(per_tile):
-                        shift_chunk(
-                            d, ref + 1, later_shift,
-                            pl.multiple_of((number * per_tile + each) * chunk, chunk),
+            shift_chunk(d, 0, shifted[0], pl.multiple_of(number * chunk, chunk))
+
+        shift_edge(d, 0, shifted[0])
+        own_tile = me * share_rows // tile
+        own_group = lax.rem(me * share_rows, tile) // group
+        for turn in range(tiles):
+            tile_start = pl.multiple_of(lax.rem(own_tile + 1 + turn, tiles) * tile, tile)
+            for ref in range(3):
+                if turn == 0 and ref < 2:
+                    part_rows = tile // 2
+
+                    @pl.loop(0, 2)
+                    def _(side):
+                        inner = pl.multiple_of(side * part_rows, part_rows)
+                        real, imag = multiply(
+                            table_i, shifted[ref], pl.ds(tile_start + inner, part_rows)
                         )
-
-            if ref < 2:
-                shift_edge(d, ref + 1, later_shift)
-            for which in range(2):
-                for start in range(0, rows_x, tile):
-                    rows = pl.ds(start, tile)
+                        returned[pl.ds(inner, part_rows), :] = real.astype(jnp.bfloat16)
+                        returned[pl.ds(tile + inner, part_rows), :] = imag.astype(jnp.bfloat16)
+                        for each in range(middle // chunk // 2):
+                            shift_chunk(
+                                d, ref + 1, shifted[ref + 1],
+                                pl.multiple_of(side * (middle // 2) + each * chunk, chunk),
+                            )
+
+                    shift_edge(d, ref + 1, shifted[ref + 1])
+                else:
+                    real, imag = multiply(table_i, shifted[ref], pl.ds(tile_start, tile))
+                    returned[:tile, :] = real.astype(jnp.bfloat16)
+                    returned[tile:, :] = imag.astype(jnp.bfloat16)
+                for which in range(2):
                     both = jnp.concatenate(
-                        [
-                            returned[rows, lanes(which)],
-                            returned[pl.ds(rows_x + start, tile), lanes(which)],
-                        ],
-                        axis=1,
+                        [returned[:tile, lanes(which)], returned[tile:, lanes(which)]], axis=1
                     )
-                    refocused[ref, which, rows, :] = jnp.dot(
+                    refocused[ref, which] = jnp.dot(
                         both, table_y[...], preferred_element_type=jnp.float32
                     )
-            if d == 0 and ref == 0:
-                begin_last(0)
-                for later in range(1, depths):
-                    begin_gather(later)
-            if d == 0 and ref == 1:
-                for later in range(1, depths):
-                    begin_last(later)
+                if d == 0 and turn == 0 and ref == 0:
+                    begin_last(0)
+                if d == 0 and turn == 0 and ref == 1:
+                    for later in range(1, depths):
+                        begin_gather(later)
+                if d == 0 and turn == tiles - 1 and ref == 1:
+                    for later in range(1, depths):
+                        begin_last(later)
+            if d == 0 and turn == 0:
+                swap_last(0).wait()
+
+            def send_group(index):
+                for each in range(group // share_rows):
+                    to = (tile_start + index * group) // share_rows + each
+                    hop = lax.rem(to - me + devices, devices)
+
+                    @pl.when(hop != 0)
+                    def _():
+                        send_cross(d, hop).start()
+
+            def turn_index(number):
+                return lax.rem(own_group + 1 + number, groups)
+
+            @pl.loop(0, groups)
+            def _(number):
+                for each in range(group // chunk):
+                    inside = pl.multiple_of(turn_index(number) * group + each * chunk, chunk)
+                    mix(d, inside, pl.multiple_of(tile_start + inside, chunk))
+
+                @pl.when(number > 0)
+                def _():
+                    send_group(turn_index(number - 1))
+
+            send_group(turn_index(groups - 1))
+
         if d == 0:
-            for each in range(depths):
-                swap_last(each).wait()
-
-        @pl.loop(0, rows_x // chunk)
-        def _(number):
-            start = pl.multiple_of(number * chunk, chunk)
-            rows = pl.ds(start, chunk)
-            slowness = slow_rows(d, start)
-            lower = bracket[d, rows, :] == 0
-            slow_low = jnp.where(lower, references[d][0], references[d][1])
-            slow_gap = jnp.where(
-                lower, references[d][1] - references[d][0], references[d][2] - references[d][1]
-            )
-            weight = jnp.clip((slowness - slow_low) / slow_gap, 0.0, 1.0)
-            sine, cosine = sin_cos((angular * layer_thick) * slowness)
-            rounded = []
-            for which in range(2):
-                mixed = []
-                for side in range(2):
-                    first = refocused[0, which, rows, lanes(side)]
-                    second = refocused[1, which, rows, lanes(side)]
-                    third = refocused[2, which, rows, lanes(side)]
-                    low = jnp.where(lower, first, second)
-                    high = jnp.where(lower, second, third)
-                    mixed.append((1.0 - weight) * low + weight * high)
-                turned = signs[which] * sine
-                real = (cosine * mixed[0] + turned * mixed[1]).astype(jnp.bfloat16)
-                imag = (turned * mixed[0] - cosine * mixed[1]).astype(jnp.bfloat16)
-                if d < depths - 1:
-                    fields[which, 0, rows, :] = real
-                    fields[which, 1, rows, :] = imag
-                rounded.append((real.astype(jnp.float32), imag.astype(jnp.float32)))
-            (sr, si), (rr, ri) = rounded
-            store_cross(d, start, 0, sr * rr + si * ri)
-            store_cross(d, start, 1, sr * ri - si * rr)
-
-        @pl.loop(1, devices)
-        def _(hop):
-            send_cross(d, hop).start()
-
+            for later in range(1, depths):
+                swap_last(later).wait()
         received[d, me] = cross[d, me]
     for d in range(depths):
         @pl.loop(1, devices)
@@ -396,8 +424,9 @@
             pltpu.VMEM((2 * rows_x, 2 * cols_y), jnp.float32),
             pltpu.VMEM((3 * rows_x, 2 * cols_y), jnp.bfloat16),
             pltpu.VMEM((3 * rows_x, 2 * cols_y), jnp.bfloat16),
-            pltpu.VMEM((2 * rows_x, 2 * cols_y), jnp.bfloat16),
-            pltpu.VMEM((3, 2, rows_x, 2 * cols_y), jnp.float32),
+            pltpu.VMEM((3 * rows_x, 2 * cols_y), jnp.bfloat16),
+            pltpu.VMEM((2 * tile, 2 * cols_y), jnp.bfloat16),
+            pltpu.VMEM((3, 2, tile, 2 * cols_y), jnp.float32),
             pltpu.VMEM((2, 2, rows_x, cols_y), jnp.bfloat16),
             pltpu.VMEM((depths, devices, 2, share_rows, cols_y), jnp.bfloat16),
             pltpu.VMEM(held, jnp.bfloat16),

time: 72.3 us -> 70 us (0.968)
  the two profiles are of different devices: /device:TPU:9 before, /device:TPU:0 now
where the time goes in v4:
time: 70 us; the launch traced here: 69.2 us
  Pallas kernels  67.8 us (97%)
  other arithmetic  0.81 us (1%)
    pallas_call x1, Pallas kernels, cross_spectra(): pl.pallas_call(functools.partial(window_kernel, devices), out_shape=jax.S...  55.9 us
    pallas_call x1, Pallas kernels, lag_image(): pl.pallas_call(functools.partial(image_kernel, slots ** (-0.5)), out_shap...  9.2 us
    pallas_call x1, Pallas kernels, cut_windows(): pl.pallas_call(functools.partial(cut_kernel, slab_count), out_shape=jax.S...  2.64 us

profile of v4, /device:TPU:0, one launch (start us, length us, event | category | flops | bytes accessed | tf_op | source)
XLA Modules:
  0.0 69.2 jit_solution(519067603147439517)
XLA Ops:
  0.0 0.8 %cosine_convert_fusion = (bf16[1,16,256]{2,1,0:T(8,128)(2,1)S(1)}, bf16[1,16,256]{2,1,0:T(8,128)(2,1)S(1)}) fusion(s32[256]{0:T(256)S(1)} %iota_add_fusion, s32[16]{0:T(128)} %bins.1), kind=kLoop, calls=%fused_computation.5 | loop fusion | flops 49152 | bytes 17472 | tf_op jit(solution)/shard_map/convert
  0.8 0.6 reshape.123.weights
  1.5 2.6 %shard_map.109 = bf16[2,512,256]{2,1,0:T(8,128)(2,1)} custom-call(s32[2]{0:T(128)} %slab_map.1, s32[2]{0:T(128)} %corner.1, bf16[1,768,512]{2,1,0:T(8,128)(2,1)} %slab.1), custom_call_target="tpu_custom_call" | custom-call | tf_op jit(solution)/shard_map/pallas_call | solution.py:486
  4.1 55.9 %shard_map.110.crosses = bf16[2,16,2,32,256]{4,3,2,1,0:T(8,128)(2,1)} custom-call(s32[16]{0:T(128)} %bins.1, f32[2,3]{1,0:T(2,128)} %gaps.1, bf16[2,512,256]{2,1,0:T(8,128)(2,1)} %bitcast.6, bf16[2,512,256]{2,1,0:T(8,128)(2,1)} %bitcast.7, bf16[512,1024]{1,0:T(8,128)(2,1)} %constant.23.clone.table_f, bf16[512,1024]{1,0:T(8,128)(2,1)} %constant.24.clone.table_i, ...), custom_call_target="tpu_custom_call" | custom-call | flops 51539607552 | bytes 8388608 | tf_op jit(solution)/shard_map/pallas_call | solution.py:417
  60.0 9.2 %shard_map.111 = f32[2,32,256,256]{3,2,1,0:T(8,128)} custom-call(bf16[2,16,2,32,256]{4,3,2,1,0:T(8,128)(2,1)} %shard_map.110.crosses, bf16[32,256]{1,0:T(8,128)(2,1)} %reshape.123.weights), custom_call_target="tpu_custom_call" | custom-call | tf_op jit(solution)/shard_map/pallas_call | solution.py:518
  (3 shorter events, 0.0 us)
